TPU v7x, 32 devices: a whole 2x2x4 slice. The times are simulated.
32 devices in a mesh: curve: 8 (over z, x), sub: 4 (over y, core).
Axes of the slice: x: 2, y: 2, z: 4, core: 2. Of those that a mesh axis runs over, the one named last changes fastest.
Arguments:
- direction: float32 [8, 4096], P(None, ('curve', 'sub')), may hold values from -6 to 6
- base_velocity: float32 [3, 16384], P(None, ('curve', 'sub')), may hold values from -6 to 6
- weight: float32 [3, 16384], P(None, ('curve', 'sub')), may hold values from 0.3 to 3
- element_matrix: float32 [81, 81, 4096], P(None, None, ('curve', 'sub')), as said below
- connectivity: int32 [27, 4096], P(None, ('curve', 'sub')), may hold values from 384 to 1151, as said below
- element_count: int32 [32], P(('curve', 'sub')), may hold values from 64 to 128
- basal_owner: int32 [8192], P(('curve', 'sub')), may hold values from 0 to 511
Outputs:
- gradient: float32 [8, 4096], P(None, ('curve', 'sub'))
- adjoint_field: float32 [3, 8, 16384], P(None, None, ('curve', 'sub'))
Inputs may be any that keep to these rules, and one draw needn't show every extreme that they name: `connectivity`: device 0 has no corner below 512 and the last device none at or above 1024. A corner below 512 is at or above 384; a corner at or above 1024 is below 1152. `element_matrix`: Symmetric.
All inputs are finite; a program needn't handle non-finite values.
Results may differ from a plain program's by a relative error of at most 0.00016.
Values sent between devices are 32-bit elements; how exact they have to be, the bound alone decides.
No kernel may reach another device: no remote copies, remote signals or barrier semaphores. Data moves between devices by JAX's collectives and lax.ppermute only.
A program may use at most 64 MiB of HBM per device.

v0:
```python
import functools

import jax
import jax.numpy as jnp
from jax import lax
from jax.experimental import pallas as pl
from jax.experimental.pallas import tpu as pltpu
from jax.sharding import PartitionSpec as P

BAND = 128
LANE = 128
AX = ("curve", "sub")
VMEM = pl.BlockSpec(memory_space=pltpu.VMEM)
SMEM = pl.BlockSpec(memory_space=pltpu.SMEM)
f32 = jnp.float32


def params(mib):
    return pltpu.CompilerParams(vmem_limit_bytes=mib << 20)


def xor_order(subs):
    order, masks = [0], []
    while len(order) < subs:
        mask = 2 * len(order) - 1
        masks.append(mask)
        order = order + [mask ^ r for r in order]
    return order, masks


def chain_mask(step, masks):
    return masks[step]


def pack_kernel(direction, velocity, owner, out):
    out[0:8, :] = direction[...]
    out[8:11, :] = velocity[:, :BAND]
    out[11:12, :] = owner[:, :BAND].astype(f32)
    out[12:16, :] = jnp.zeros((4, LANE), f32)


def grow_kernel(held, got, out):
    dirs = held.shape[0] - 8
    out[0:dirs, :] = held[0:dirs, :]
    out[dirs : 2 * dirs, :] = got[0:dirs, :]
    out[2 * dirs : 2 * dirs + 8, :] = held[dirs : dirs + 8, :]


def rows8(row):
    return jnp.broadcast_to(row, (8, LANE))


def lanes_of(table, index):
    return jnp.take_along_axis(table, index, axis=1, mode="promise_in_bounds")


def lookup(owner_row, tables, shards):
    low = rows8(owner_row & (LANE - 1))
    high = rows8(owner_row >> 7)
    out = jnp.zeros((8, LANE), f32)
    for table, shard in zip(tables, shards):
        out = jnp.where(high == shard, lanes_of(table, low), out)
    return out


def gather_corners(field, blocks, conn, base, corners, v_ref):
    held = {(c, b): field(c, b) for c in range(3) for b in blocks}
    for n in range(corners):
        row = conn[n : n + 1, :] - base
        low = rows8(row & (LANE - 1))
        high = rows8(row >> 7)
        tests = {b: high == b for b in blocks}
        for c in range(3):
            acc = jnp.zeros((8, LANE), f32)
            for b in blocks:
                acc = jnp.where(tests[b], lanes_of(held[c, b], low), acc)
            v_ref[c * corners + n] = acc


def product(k_ref, v_ref, o_ref, count, size, group=9):
    live = (lax.broadcasted_iota(jnp.int32, (8, LANE), 1) < count).astype(f32)

    def step(i, carry):
        start = i * group
        acc = [jnp.zeros((8, LANE), f32) for _ in range(group)]
        for j in range(size):
            vj = v_ref[j]
            for t in range(group):
                acc[t] = acc[t] + rows8(k_ref[start + t, j : j + 1, :]) * vj
        for t in range(group):
            o_ref[start + t] = acc[t] * live
        return carry

    lax.fori_loop(0, size // group, step, 0)


def halves(x):
    high = x.astype(jnp.bfloat16).astype(f32)
    return high, x - high


def scatter_corners(o_ref, conn, base, corners, blocks, a_ref, one_ref):
    sub = lax.broadcasted_iota(jnp.int32, (LANE, LANE), 0)
    for n in range(corners):
        row = conn[n : n + 1, :] - base
        low = jnp.broadcast_to(row & (LANE - 1), (LANE, LANE))
        one_ref[:, n * LANE : (n + 1) * LANE] = (low == sub).astype(f32).astype(jnp.bfloat16)
        high = rows8(row >> 7)
        parts = [halves(o_ref[c * corners + n]) for c in range(3)]
        pieces = [p[0] for p in parts] + [p[1] for p in parts]
        for b in range(blocks):
            here = high == b
            stack = jnp.concatenate([jnp.where(here, p, 0.0) for p in pieces], axis=0)
            a_ref[b * 48 : (b + 1) * 48, n * LANE : (n + 1) * LANE] = stack.astype(jnp.bfloat16)
    res = lax.dot_general(
        a_ref[...], one_ref[...], (((1,), (1,)), ((), ())), preferred_element_type=f32
    )
    return [res[b * 48 : b * 48 + 24] + res[b * 48 + 24 : b * 48 + 48] for b in range(blocks)]


def pick(index, options):
    out = options[-1][1]
    for value, array in options[:-1]:
        out = jnp.where(index == value, array, out)
    return out


def forward_kernel(cfg, *refs):
    subs, order, masks, nodes, basal, corners = cfg
    steps = len(masks)
    held, got, (low_b, mid_b) = refs[0], refs[1 : 1 + steps], refs[1 + steps : 3 + steps]
    velocity, owner, weight, kmat, conn, count = refs[3 + steps : 9 + steps]
    ext, m0, m1, info_out = refs[9 + steps : 13 + steps]
    v_ref, o_ref, a_ref, one_ref = refs[13 + steps :]
    s = lax.axis_index("sub")
    half = subs // 2
    own_blocks = nodes // LANE
    blocks = own_blocks + 2
    last = s == subs - 1
    dirs = 8 * half

    info = low_b[dirs : dirs + 8, :]
    for t in range(steps):
        rows = got[t].shape[0]
        chain = (s & (2 * (1 << t) - 1)) == (1 << t) - 1
        info = jnp.where(chain, got[t][rows - 8 : rows, :], info)
    info = jnp.where(last, low_b[dirs : dirs + 8, :], info)
    info_out[...] = info

    mine = [held[8 * q : 8 * q + 8, :] for q in range(half)]
    mine += [got[-1][8 * q : 8 * q + 8, :] for q in range(half)]
    shards = [s ^ r for r in order]
    theirs = [low_b[8 * q : 8 * q + 8, :] for q in range(half)]
    theirs += [mid_b[8 * q : 8 * q + 8, :] for q in range(half)]
    their_shards = [order[q] for q in range(half)] + [half ^ order[q] for q in range(half)]
    next_tables = [jnp.where(last, b, a) for a, b in zip(mine, theirs)]
    next_shards = [jnp.where(last, b, a) for a, b in zip(shards, their_shards)]

    values = {}
    for b in range(basal // LANE):
        beta = lookup(owner[:, b * LANE : (b + 1) * LANE], mine, shards)
        for c in range(3):
            values[c, 1 + b] = rows8(velocity[c : c + 1, b * LANE : (b + 1) * LANE]) * beta
    beta = lookup(info[3:4, :].astype(jnp.int32), next_tables, next_shards)
    for c in range(3):
        values[c, blocks - 1] = rows8(info[c : c + 1, :]) * beta
    live_blocks = [1 + b for b in range(basal // LANE)] + [blocks - 1]
    base = nodes - BAND
    gather_corners(lambda c, b: values[c, b], live_blocks, conn, base, corners, v_ref)
    product(kmat, v_ref, o_ref, count[0], 3 * corners)
    sums = scatter_corners(o_ref, conn, base, corners, blocks, a_ref, one_ref)
    for b in range(blocks):
        ext[:, b * LANE : (b + 1) * LANE] = sums[b]
    even = (s & 1) == 0
    before = jnp.concatenate([sums[0], sums[1]], axis=1)
    after = jnp.concatenate([sums[blocks - 2], sums[blocks - 1]], axis=1)
    m0[0:24, :] = jnp.where(even, after, before)
    m1[0:24, :] = jnp.where(even, before, after)
    pad = jnp.zeros((5, LANE), f32)
    none = jnp.zeros((8, LANE), f32)
    w_low = jnp.concatenate([weight[:, 0:BAND], pad], axis=0)
    w_high = jnp.concatenate([weight[:, nodes - BAND : nodes], pad], axis=0)
    before = jnp.concatenate([none, w_low], axis=1)
    after = jnp.concatenate([w_high, none], axis=1)
    m0[24:32, :] = jnp.where(even, after, before)
    m1[24:32, :] = jnp.where(even, before, after)


def adjoint_kernel(cfg, *refs):
    subs, order, masks, nodes, basal, corners = cfg
    ext, r0, r1, info, velocity, owner, weight, kmat, conn, count = refs[:10]
    n_out = 4 + len(masks)
    outs = refs[10 : 10 + n_out]
    v_ref, o_ref, a_ref, one_ref = refs[10 + n_out :]
    own_out, swap_out, edge_out, mid_out = outs[:4]
    dense_out = outs[4]
    band_outs = outs[5:]
    s = lax.axis_index("sub")
    half = subs // 2
    blocks = nodes // LANE + 2
    last = s == subs - 1
    even = (s & 1) == 0
    base = nodes - BAND

    prev = jnp.where(even, r1[...], r0[...])
    nxt = jnp.where(even, r0[...], r1[...])

    values = {}
    for c in range(3):
        part = slice(8 * c, 8 * c + 8)
        for b in range(blocks):
            x = ext[part, b * LANE : (b + 1) * LANE]
            if b == 0:
                x = (x + prev[part, 0:LANE]) * rows8(prev[24 + c : 25 + c, 0:LANE])
            elif b == blocks - 1:
                x = (x + nxt[part, LANE:]) * rows8(nxt[24 + c : 25 + c, LANE:])
            else:
                if b == 1:
                    x = x + prev[part, LANE:]
                if b == blocks - 2:
                    x = x + nxt[part, 0:LANE]
                x = x * rows8(weight[c : c + 1, (b - 1) * LANE : b * LANE])
            values[c, b] = x
    gather_corners(lambda c, b: values[c, b], range(blocks), conn, base, corners, v_ref)
    product(kmat, v_ref, o_ref, count[0], 3 * corners)
    sums = scatter_corners(o_ref, conn, base, corners, blocks, a_ref, one_ref)
    for b in range(1, blocks - 1):
        own_out[:, (b - 1) * LANE : b * LANE] = sums[b]
    lower, upper = sums[0], sums[blocks - 1]

    n_basal = basal // LANE
    terms, owners = [], []
    for b in range(n_basal):
        terms.append(
            sum(
                rows8(velocity[c : c + 1, b * LANE : (b + 1) * LANE]) * sums[1 + b][8 * c : 8 * c + 8]
                for c in range(3)
            )
        )
        owners.append(owner[:, b * LANE : (b + 1) * LANE])
    beyond = sum(rows8(info[c : c + 1, :]) * upper[8 * c : 8 * c + 8] for c in range(3))
    terms.append(jnp.where(last, 0.0, beyond))
    owners.append(info[3:4, :].astype(jnp.int32))
    across = jnp.where(last, beyond, 0.0)
    sub_iota = lax.broadcasted_iota(jnp.int32, (LANE, LANE), 0)
    one = jnp.concatenate(
        [
            (jnp.broadcast_to(o & (LANE - 1), (LANE, LANE)) == sub_iota).astype(f32).astype(jnp.bfloat16)
            for o in owners
        ],
        axis=1,
    )
    split = [halves(t) for t in terms]
    split_across = halves(across)
    zero = jnp.zeros((8, LANE), f32)
    lines = []
    for r in order:
        here = [rows8(o >> 7) == (s ^ r) for o in owners]
        for piece in range(2):
            lines.append(
                jnp.concatenate([jnp.where(h, t[piece], 0.0) for h, t in zip(here, split)], axis=1)
            )
    for q in range(subs):
        shard = order[q] if q < half else half ^ order[q - half]
        here = rows8(owners[-1] >> 7) == shard
        for piece in range(2):
            lines.append(
                jnp.concatenate(
                    [zero] * n_basal + [jnp.where(here, split_across[piece], 0.0)], axis=1
                )
            )
    res = lax.dot_general(
        jnp.concatenate(lines, axis=0).astype(jnp.bfloat16),
        one,
        (((1,), (1,)), ((), ())),
        preferred_element_type=f32,
    )
    dense = [res[16 * q : 16 * q + 8] + res[16 * q + 8 : 16 * q + 16] for q in range(2 * subs)]
    rows = 8 * half
    for q in range(half):
        dense_out[8 * q : 8 * q + 8, :] = dense[q]
        swap_out[8 * q : 8 * q + 8, :] = dense[half + q]
        edge_out[8 * q : 8 * q + 8, :] = dense[subs + q]
        mid_out[8 * q : 8 * q + 8, :] = dense[subs + half + q]
    edge_out[rows : rows + 24, :] = jnp.where(last, upper, lower)
    up = (s & half) == 0
    swap_out[rows : rows + 24, :] = jnp.where(up, upper, lower)
    for t, band in enumerate(band_outs):
        up = (s & (1 << t)) == 0
        band[...] = jnp.where(up, upper, lower)


def shrink_kernel(first, *refs):
    if first:
        held, got, edge, mid, band, msg, left = refs
    else:
        held, got, band, msg, left = refs
    rows = held.shape[0]
    total = held[...] + got[0:rows, :]
    if first:
        total = total + edge[0:rows, :] + mid[...]
    keep = rows // 2
    left[...] = total[0:keep]
    msg[0:keep, :] = total[keep:]
    msg[keep : keep + 24, :] = band[...]


def finish_kernel(cfg, *refs):
    subs, order, masks, nodes, basal, corners = cfg
    steps = len(masks)
    own, held, edge = refs[:3]
    got = refs[3 : 3 + steps]
    gradient, field = refs[3 + steps :]
    s = lax.axis_index("sub")
    gradient[...] = held[...] + got[0][0:8, :]
    bands = [g[g.shape[0] - 24 :, :] for g in got]
    prev = edge[edge.shape[0] - 24 :, :]
    nxt = prev
    for t in range(steps):
        ones = (1 << t) - 1
        nxt = jnp.where((s & (2 * ones + 1)) == ones, bands[t], nxt)
        prev = jnp.where((s & (2 * ones + 1)) == ones + 1, bands[t], prev)
    field[:, 0:LANE] = own[:, 0:LANE] + prev
    field[:, LANE : nodes - LANE] = own[:, LANE : nodes - LANE]
    field[:, nodes - LANE :] = own[:, nodes - LANE :] + nxt


def shape(*dims):
    return jax.ShapeDtypeStruct(dims, f32)


def local(curves, subs, direction, base_velocity, weight, element_matrix, connectivity, element_count, basal_owner):
    order, masks = xor_order(subs)
    total = curves * subs
    half = subs // 2
    nodes = base_velocity.shape[1]
    basal = basal_owner.shape[0]
    corners, elems = connectivity.shape
    size = 3 * corners
    blocks = nodes // LANE + 2
    cfg = (subs, order, masks, nodes, basal, corners)
    owner = basal_owner.reshape(1, basal)

    def call(kernel, out_shape, scratch=(), mib=4, specs=None):
        def run(*args):
            return pl.pallas_call(
                kernel,
                out_shape=out_shape,
                in_specs=specs or [VMEM] * len(args),
                out_specs=jax.tree.map(lambda _: VMEM, out_shape),
                scratch_shapes=list(scratch),
                compiler_params=params(mib),
            )(*args)

        return run

    def swap_sub(x, mask):
        return lax.ppermute(x, "sub", [(i, i ^ mask) for i in range(subs)])

    edges = [(subs * g + subs - 1, subs * (g + 1)) for g in range(curves - 1)]

    held = call(pack_kernel, shape(16, LANE))(direction, base_velocity, owner)
    got = []
    for mask in masks[:-1]:
        got.append(swap_sub(held, mask))
        rows = 2 * held.shape[0] - 8
        held = call(grow_kernel, shape(rows, LANE))(held, got[-1])
    got.append(swap_sub(held, masks[-1]))
    low_b = lax.ppermute(held, AX, [(b, a) for a, b in edges])
    mid_b = lax.ppermute(held, AX, [(b + half, a) for a, b in edges])

    scratch = [
        pltpu.VMEM((size, 8, LANE), f32),
        pltpu.VMEM((size, 8, LANE), f32),
        pltpu.VMEM((48 * blocks, corners * LANE), jnp.bfloat16),
        pltpu.VMEM((LANE, corners * LANE), jnp.bfloat16),
    ]
    ext, m0, m1, info = call(
        functools.partial(forward_kernel, cfg),
        (shape(24, blocks * LANE), shape(32, 2 * LANE), shape(32, 2 * LANE), shape(8, LANE)),
        scratch,
        16,
        [VMEM] * (8 + len(got)) + [SMEM],
    )(held, *got, low_b, mid_b, base_velocity, owner, weight, element_matrix, connectivity, element_count)

    r0 = lax.ppermute(m0, AX, [p for i in range(0, total - 1, 2) for p in ((i, i + 1), (i + 1, i))])
    r1 = lax.ppermute(m1, AX, [p for i in range(1, total - 1, 2) for p in ((i, i + 1), (i + 1, i))])

    steps = len(masks)
    rows = 8 * half
    own, swap_msg, edge_msg, mid_msg, dense, *bands = call(
        functools.partial(adjoint_kernel, cfg),
        (shape(24, nodes), shape(rows + 24, LANE), shape(rows + 24, LANE), shape(rows, LANE), shape(rows, LANE))
        + (shape(24, LANE),) * (steps - 1),
        scratch,
        16,
        [VMEM] * 9 + [SMEM],
    )(ext, r0, r1, info, base_velocity, owner, weight, element_matrix, connectivity, element_count)

    by_mask = [None] * steps
    by_mask[-1] = swap_sub(swap_msg, masks[-1])
    edge = lax.ppermute(edge_msg, AX, [p for a, b in edges for p in ((a, b), (b, a))])
    mid = lax.ppermute(mid_msg, AX, [(a, b + half) for a, b in edges])
    extra = (edge, mid)
    for t in range(steps - 2, -1, -1):
        keep = dense.shape[0] // 2
        msg, dense = call(
            functools.partial(shrink_kernel, bool(extra)), (shape(keep + 24, LANE), shape(keep, LANE))
        )(dense, by_mask[t + 1], *extra, bands[t])
        extra = ()
        by_mask[t] = swap_sub(msg, masks[t])
    gradient, field = call(functools.partial(finish_kernel, cfg), (shape(8, LANE), shape(24, nodes)))(
        own, dense, edge, *by_mask
    )
    return gradient, field.reshape(3, 8, nodes)


def solution(mesh):
    curves, subs = mesh.shape["curve"], mesh.shape["sub"]
    in_specs = (
        P(None, AX),
        P(None, AX),
        P(None, AX),
        P(None, None, AX),
        P(None, AX),
        P(AX),
        P(AX),
    )
    out_specs = (P(None, AX), P(None, None, AX))
    return jax.shard_map(
        functools.partial(local, curves, subs), mesh=mesh, in_specs=in_specs, out_specs=out_specs, check_vma=False
    )
```

profile of v0, /device:TPU:15, one launch (start us, length us, event | category | flops | bytes accessed | tf_op | source)
XLA Modules:
  0.0 43.4 jit_solution(5178068422352417783)
XLA Ops:
  0.6 0.0 copy-start.2
  0.6 0.7 %copy-done.2 = f32[3,512]{1,0:T(4,128)S(1)} copy-done((f32[3,512]{1,0:T(4,128)S(1)}, f32[3,512]{1,0:T(4,128)}, u32[]{:S(2)}) %copy-start.2) | copy-done | bytes 6168
  1.3 0.0 copy-start.7
  1.3 0.7 %copy-done.7 = s32[256]{0:T(256)S(1)} copy-done((s32[256]{0:T(256)S(1)}, s32[256]{0:T(256)}, u32[]{:S(2)}) %copy-start.7) | copy-done | bytes 1048
  2.0 0.0 copy-start.9
  2.0 0.7 %copy-done.9 = f32[8,128]{1,0:T(8,128)S(1)} copy-done((f32[8,128]{1,0:T(8,128)S(1)}, f32[8,128]{1,0:T(8,128)}, u32[]{:S(2)}) %copy-start.9) | copy-done | bytes 4120
  2.7 0.0 copy-start.5
  2.7 0.7 %collective-permute-start = (f32[16,128]{1,0:T(8,128)S(1)}, f32[16,128]{1,0:T(8,128)S(1)}, u32[]{:S(2)}, u32[]{:S(2)}) collective-permute-start(f32[16,128]{1,0:T(8,128)S(1)} %shard_map.86.held), channel_id=1, source_target_pairs={{0,1},{1,0},{2,3},{3,2},{4,5},{5,4},{6,7},{7,6},{8,9},{9,8},{10,11... | collective-permute-start | bytes 24584 | tf_op jit(solution)/shard_map/ppermute | solution.py:358
  3.4 0.8 %collective-permute-done.got.refs_1_ = f32[16,128]{1,0:T(8,128)S(1)} collective-permute-done((f32[16,128]{1,0:T(8,128)S(1)}, f32[16,128]{1,0:T(8,128)S(1)}, u32[]{:S(2)}, u32[]{:S(2)}) %collective-permute-start) | collective-permute-done | bytes 8224 | tf_op jit(solution)/shard_map/ppermute | solution.py:358
  4.2 1.3 %collective-permute-start.3 = (f32[24,128]{1,0:T(8,128)S(1)}, f32[24,128]{1,0:T(8,128)S(1)}, u32[]{:S(2)}, u32[]{:S(2)}) collective-permute-start(f32[24,128]{1,0:T(8,128)S(1)} %shard_map.87.refs_0_), channel_id=1, source_target_pairs={{6,3},{10,7},{14,11},{18,15},{22,19},{26,23},{30,27}} | collective-permute-start | bytes 36872 | tf_op jit(solution)/shard_map/ppermute | solution.py:370
  5.5 1.3 %collective-permute-start.2 = (f32[24,128]{1,0:T(8,128)S(1)}, f32[24,128]{1,0:T(8,128)S(1)}, u32[]{:S(2)}, u32[]{:S(2)}) collective-permute-start(f32[24,128]{1,0:T(8,128)S(1)} %shard_map.87.refs_0_), channel_id=1, source_target_pairs={{4,3},{8,7},{12,11},{16,15},{20,19},{24,23},{28,27}} | collective-permute-start | bytes 36872 | tf_op jit(solution)/shard_map/ppermute | solution.py:369
  6.8 2.4 %collective-permute-start.1 = (f32[24,128]{1,0:T(8,128)S(1)}, f32[24,128]{1,0:T(8,128)S(1)}, u32[]{:S(2)}, u32[]{:S(2)}) collective-permute-start(f32[24,128]{1,0:T(8,128)S(1)} %shard_map.87.refs_0_), channel_id=1, source_target_pairs={{0,3},{1,2},{2,1},{3,0},{4,7},{5,6},{6,5},{7,4},{8,11},{9,10},{10,... | collective-permute-start | bytes 36872 | tf_op jit(solution)/shard_map/ppermute | solution.py:358
  9.8 0.3 collective-permute-done.3.refs_4_
  10.1 2.2 %collective-permute-done.2.refs_3_ = f32[24,128]{1,0:T(8,128)S(1)} collective-permute-done((f32[24,128]{1,0:T(8,128)S(1)}, f32[24,128]{1,0:T(8,128)S(1)}, u32[]{:S(2)}, u32[]{:S(2)}) %collective-permute-start.2) | collective-permute-done | bytes 12320 | tf_op jit(solution)/shard_map/ppermute | solution.py:369
  12.3 0.0 collective-permute-done.1.refs_2_
  12.3 0.0 copy-start
  12.3 2.0 %copy-done = f32[81,81,128]{2,1,0:T(8,128)S(1)} copy-done((f32[81,81,128]{2,1,0:T(8,128)S(1)}, f32[81,81,128]{2,1,0:T(8,128)}, u32[]{:S(2)}) %copy-start) | copy-done | bytes 3359256
  14.3 0.0 copy-start.3
  14.4 0.7 %copy-done.3 = f32[3,512]{1,0:T(4,128)S(1)} copy-done((f32[3,512]{1,0:T(4,128)S(1)}, f32[3,512]{1,0:T(4,128)}, u32[]{:S(2)}) %copy-start.3) | copy-done | bytes 6168
  15.0 0.0 copy-start.4
  15.0 0.7 %copy-done.4 = s32[27,128]{1,0:T(8,128)S(1)} copy-done((s32[27,128]{1,0:T(8,128)S(1)}, s32[27,128]{1,0:T(8,128)}, u32[]{:S(2)}) %copy-start.4) | copy-done | bytes 13848
  15.8 0.0 copy-start.6
  15.8 0.7 %copy-done.6 = f32[3,512]{1,0:T(4,128)S(1)} copy-done((f32[3,512]{1,0:T(4,128)S(1)}, f32[3,512]{1,0:T(4,128)}, u32[]{:S(2)}) %copy-start.6) | copy-done | bytes 6168
  16.5 0.0 copy-start.8
  16.5 0.7 %copy-done.8 = s32[256]{0:T(256)S(1)} copy-done((s32[256]{0:T(256)S(1)}, s32[256]{0:T(256)}, u32[]{:S(2)}) %copy-start.8) | copy-done | bytes 1048
  17.1 0.0 copy-start.1
  17.1 4.8 %shard_map.88 = (f32[24,768]{1,0:T(8,128)S(1)}, f32[32,256]{1,0:T(8,128)S(1)}, f32[32,256]{1,0:T(8,128)S(1)}, f32[8,128]{1,0:T(8,128)S(1)}) custom-call(f32[24,128]{1,0:T(8,128)S(1)} %shard_map.87.refs_0_, f32[16,128]{1,0:T(8,128)S(1)} %collective-permute-done.got.refs_1_, f32[24,128]{1,0:T(8,128)S(1)} %collective-permute-done.1.refs_2_, ...), custom_call_target="tpu_custom_call" | custom-call | tf_op jit(solution)/shard_map/pallas_call | solution.py:346
  21.9 0.1 collective-permute-start.4
  22.0 3.7 %collective-permute-start.5 = (f32[32,256]{1,0:T(8,128)S(1)}, f32[32,256]{1,0:T(8,128)S(1)}, u32[]{:S(2)}, u32[]{:S(2)}) collective-permute-start(f32[32,256]{1,0:T(8,128)S(1)} %get-tuple-element.18), channel_id=1, source_target_pairs={{1,2},{2,1},{3,4},{4,3},{5,6},{6,5},{7,8},{8,7},{9,10},{10,9},{11,... | collective-permute-start | bytes 98312 | tf_op jit(solution)/shard_map/ppermute | solution.py:387
  25.7 0.0 collective-permute-done.4.refs_1_
  25.7 3.3 %collective-permute-done.5.refs_2_ = f32[32,256]{1,0:T(8,128)S(1)} collective-permute-done((f32[32,256]{1,0:T(8,128)S(1)}, f32[32,256]{1,0:T(8,128)S(1)}, u32[]{:S(2)}, u32[]{:S(2)}) %collective-permute-start.5) | collective-permute-done | bytes 32800 | tf_op jit(solution)/shard_map/ppermute | solution.py:387
  29.0 0.0 copy-done.5
  29.0 0.0 copy-done.1
  29.0 4.9 %shard_map.89 = (f32[24,512]{1,0:T(8,128)S(1)}, f32[40,128]{1,0:T(8,128)S(1)}, f32[40,128]{1,0:T(8,128)S(1)}, f32[16,128]{1,0:T(8,128)S(1)}, f32[16,128]{1,0:T(8,128)S(1)}, /*index=5*/f32[24,128]{1,0:T(8,128)S(1)}) custom-call(f32[24,768]{1,0:T(8,128)S(1)} %get-tuple-element.16.refs_0_, f32[32,256]{1,0:T(8,128)S(1)} %collective-permute-done.4.refs_1_, ...), custom_call_target="tpu_custom_call" | custom-call | tf_op jit(solution)/shard_map/pallas_call | solution.py:346
  34.0 0.1 collective-permute-start.6
  34.0 3.7 %collective-permute-start.7 = (f32[40,128]{1,0:T(8,128)S(1)}, f32[40,128]{1,0:T(8,128)S(1)}, u32[]{:S(2)}, u32[]{:S(2)}) collective-permute-start(f32[40,128]{1,0:T(8,128)S(1)} %get-tuple-element.23), channel_id=1, source_target_pairs={{3,4},{4,3},{7,8},{8,7},{11,12},{12,11},{15,16},{16,15},{19,20},{2... | collective-permute-start | bytes 61448 | tf_op jit(solution)/shard_map/ppermute | solution.py:402
  37.8 1.3 %collective-permute-start.8 = (f32[16,128]{1,0:T(8,128)S(1)}, f32[16,128]{1,0:T(8,128)S(1)}, u32[]{:S(2)}, u32[]{:S(2)}) collective-permute-start(f32[16,128]{1,0:T(8,128)S(1)} %get-tuple-element.24), channel_id=1, source_target_pairs={{3,6},{7,10},{11,14},{15,18},{19,22},{23,26},{27,30}} | collective-permute-start | bytes 24584 | tf_op jit(solution)/shard_map/ppermute | solution.py:403
  39.1 0.8 %collective-permute-done.8.refs_3_ = f32[16,128]{1,0:T(8,128)S(1)} collective-permute-done((f32[16,128]{1,0:T(8,128)S(1)}, f32[16,128]{1,0:T(8,128)S(1)}, u32[]{:S(2)}, u32[]{:S(2)}) %collective-permute-start.8) | collective-permute-done | bytes 8224 | tf_op jit(solution)/shard_map/ppermute | solution.py:403
  39.9 0.0 collective-permute-done.6.refs_1_.refs_4_
  39.9 1.1 %collective-permute-done.7.refs_2_ = f32[40,128]{1,0:T(8,128)S(1)} collective-permute-done((f32[40,128]{1,0:T(8,128)S(1)}, f32[40,128]{1,0:T(8,128)S(1)}, u32[]{:S(2)}, u32[]{:S(2)}) %collective-permute-start.7) | collective-permute-done | bytes 20512 | tf_op jit(solution)/shard_map/ppermute | solution.py:402
  41.0 1.0 %collective-permute-start.9 = (f32[32,128]{1,0:T(8,128)S(1)}, f32[32,128]{1,0:T(8,128)S(1)}, u32[]{:S(2)}, u32[]{:S(2)}) collective-permute-start(f32[32,128]{1,0:T(8,128)S(1)} %get-tuple-element.27), channel_id=1, source_target_pairs={{0,1},{1,0},{2,3},{3,2},{4,5},{5,4},{6,7},{7,6},{8,9},{9,8},{10,11... | collective-permute-start | bytes 49160 | tf_op jit(solution)/shard_map/ppermute | solution.py:358
  41.9 0.8 %collective-permute-done.9.refs_3_ = f32[32,128]{1,0:T(8,128)S(1)} collective-permute-done((f32[32,128]{1,0:T(8,128)S(1)}, f32[32,128]{1,0:T(8,128)S(1)}, u32[]{:S(2)}, u32[]{:S(2)}) %collective-permute-start.9) | collective-permute-done | bytes 16416 | tf_op jit(solution)/shard_map/ppermute | solution.py:358
  42.8 0.6 %shard_map.91 = (f32[8,128]{1,0:T(8,128)}, f32[24,512]{1,0:T(8,128)}) custom-call(f32[24,512]{1,0:T(8,128)S(1)} %get-tuple-element.20.refs_0_, f32[8,128]{1,0:T(8,128)S(1)} %get-tuple-element.26.refs_1_, f32[40,128]{1,0:T(8,128)S(1)} %collective-permute-done.7.refs_2_, f32[32,128]{1,0:T(8,128)S(1)} %collective-permute-done.9.refs_3_, ...), custom_call_target="tpu_custom_call" | custom-call | tf_op jit(solution)/shard_map/pallas_call | solution.py:346
  (3 shorter events, 0.0 us)
Async XLA Ops:
  0.6 0.7 %copy-start.2 = (f32[3,512]{1,0:T(4,128)S(1)}, f32[3,512]{1,0:T(4,128)}, u32[]{:S(2)}) copy-start(f32[3,512]{1,0:T(4,128)} %refs_4_.1) | copy-start | bytes 18436
  1.3 0.7 %copy-start.7 = (s32[256]{0:T(256)S(1)}, s32[256]{0:T(256)}, u32[]{:S(2)}) copy-start(s32[256]{0:T(256)} %param.13) | copy-start | bytes 3076
  2.0 0.7 %copy-start.9 = (f32[8,128]{1,0:T(8,128)S(1)}, f32[8,128]{1,0:T(8,128)}, u32[]{:S(2)}) copy-start(f32[8,128]{1,0:T(8,128)} %direction.1) | copy-start | bytes 12292
  2.7 26.3 %copy-start.5 = (s32[27,128]{1,0:T(8,128)S(1)}, s32[27,128]{1,0:T(8,128)}, u32[]{:S(2)}) copy-start(s32[27,128]{1,0:T(8,128)} %refs_8_.3) | copy-start | bytes 41476
  2.7 1.5 %collective-permute-start = (f32[16,128]{1,0:T(8,128)S(1)}, f32[16,128]{1,0:T(8,128)S(1)}, u32[]{:S(2)}, u32[]{:S(2)}) collective-permute-start(f32[16,128]{1,0:T(8,128)S(1)} %shard_map.86.held), channel_id=1, source_target_pairs={{0,1},{1,0},{2,3},{3,2},{4,5},{5,4},{6,7},{7,6},{8,9},{9,8},{10,11... | collective-permute-start | bytes 24584 | tf_op jit(solution)/shard_map/ppermute | solution.py:358
  4.2 5.9 %collective-permute-start.3 = (f32[24,128]{1,0:T(8,128)S(1)}, f32[24,128]{1,0:T(8,128)S(1)}, u32[]{:S(2)}, u32[]{:S(2)}) collective-permute-start(f32[24,128]{1,0:T(8,128)S(1)} %shard_map.87.refs_0_), channel_id=1, source_target_pairs={{6,3},{10,7},{14,11},{18,15},{22,19},{26,23},{30,27}} | collective-permute-start | bytes 36872 | tf_op jit(solution)/shard_map/ppermute | solution.py:370
  5.5 6.8 %collective-permute-start.2 = (f32[24,128]{1,0:T(8,128)S(1)}, f32[24,128]{1,0:T(8,128)S(1)}, u32[]{:S(2)}, u32[]{:S(2)}) collective-permute-start(f32[24,128]{1,0:T(8,128)S(1)} %shard_map.87.refs_0_), channel_id=1, source_target_pairs={{4,3},{8,7},{12,11},{16,15},{20,19},{24,23},{28,27}} | collective-permute-start | bytes 36872 | tf_op jit(solution)/shard_map/ppermute | solution.py:369
  6.8 5.5 %collective-permute-start.1 = (f32[24,128]{1,0:T(8,128)S(1)}, f32[24,128]{1,0:T(8,128)S(1)}, u32[]{:S(2)}, u32[]{:S(2)}) collective-permute-start(f32[24,128]{1,0:T(8,128)S(1)} %shard_map.87.refs_0_), channel_id=1, source_target_pairs={{0,3},{1,2},{2,1},{3,0},{4,7},{5,6},{6,5},{7,4},{8,11},{9,10},{10,... | collective-permute-start | bytes 36872 | tf_op jit(solution)/shard_map/ppermute | solution.py:358
  12.3 2.0 %copy-start = (f32[81,81,128]{2,1,0:T(8,128)S(1)}, f32[81,81,128]{2,1,0:T(8,128)}, u32[]{:S(2)}) copy-start(f32[81,81,128]{2,1,0:T(8,128)} %refs_7_.3) | copy-start | bytes 10077700
  14.3 0.7 %copy-start.3 = (f32[3,512]{1,0:T(4,128)S(1)}, f32[3,512]{1,0:T(4,128)}, u32[]{:S(2)}) copy-start(f32[3,512]{1,0:T(4,128)} %refs_4_.1) | copy-start | bytes 18436
  15.0 0.7 %copy-start.4 = (s32[27,128]{1,0:T(8,128)S(1)}, s32[27,128]{1,0:T(8,128)}, u32[]{:S(2)}) copy-start(s32[27,128]{1,0:T(8,128)} %refs_8_.3) | copy-start | bytes 41476
  15.8 0.7 %copy-start.6 = (f32[3,512]{1,0:T(4,128)S(1)}, f32[3,512]{1,0:T(4,128)}, u32[]{:S(2)}) copy-start(f32[3,512]{1,0:T(4,128)} %refs_6_.1) | copy-start | bytes 18436
  16.5 0.7 %copy-start.8 = (s32[256]{0:T(256)S(1)}, s32[256]{0:T(256)}, u32[]{:S(2)}) copy-start(s32[256]{0:T(256)} %param.13) | copy-start | bytes 3076
  17.1 11.9 %copy-start.1 = (f32[81,81,128]{2,1,0:T(8,128)S(1)}, f32[81,81,128]{2,1,0:T(8,128)}, u32[]{:S(2)}) copy-start(f32[81,81,128]{2,1,0:T(8,128)} %refs_7_.3) | copy-start | bytes 10077700
  21.9 3.8 %collective-permute-start.4 = (f32[32,256]{1,0:T(8,128)S(1)}, f32[32,256]{1,0:T(8,128)S(1)}, u32[]{:S(2)}, u32[]{:S(2)}) collective-permute-start(f32[32,256]{1,0:T(8,128)S(1)} %get-tuple-element.17), channel_id=1, source_target_pairs={{0,1},{1,0},{2,3},{3,2},{4,5},{5,4},{6,7},{7,6},{8,9},{9,8},{10,11... | collective-permute-start | bytes 98312 | tf_op jit(solution)/shard_map/ppermute | solution.py:386
  22.0 7.0 %collective-permute-start.5 = (f32[32,256]{1,0:T(8,128)S(1)}, f32[32,256]{1,0:T(8,128)S(1)}, u32[]{:S(2)}, u32[]{:S(2)}) collective-permute-start(f32[32,256]{1,0:T(8,128)S(1)} %get-tuple-element.18), channel_id=1, source_target_pairs={{1,2},{2,1},{3,4},{4,3},{5,6},{6,5},{7,8},{8,7},{9,10},{10,9},{11,... | collective-permute-start | bytes 98312 | tf_op jit(solution)/shard_map/ppermute | solution.py:387
  34.0 5.9 %collective-permute-start.6 = (f32[40,128]{1,0:T(8,128)S(1)}, f32[40,128]{1,0:T(8,128)S(1)}, u32[]{:S(2)}, u32[]{:S(2)}) collective-permute-start(f32[40,128]{1,0:T(8,128)S(1)} %get-tuple-element.22), channel_id=1, source_target_pairs={{0,3},{1,2},{2,1},{3,0},{4,7},{5,6},{6,5},{7,4},{8,11},{9,10},{10,... | collective-permute-start | bytes 61448 | tf_op jit(solution)/shard_map/ppermute | solution.py:358
  34.0 6.9 %collective-permute-start.7 = (f32[40,128]{1,0:T(8,128)S(1)}, f32[40,128]{1,0:T(8,128)S(1)}, u32[]{:S(2)}, u32[]{:S(2)}) collective-permute-start(f32[40,128]{1,0:T(8,128)S(1)} %get-tuple-element.23), channel_id=1, source_target_pairs={{3,4},{4,3},{7,8},{8,7},{11,12},{12,11},{15,16},{16,15},{19,20},{2... | collective-permute-start | bytes 61448 | tf_op jit(solution)/shard_map/ppermute | solution.py:402
  37.8 2.1 %collective-permute-start.8 = (f32[16,128]{1,0:T(8,128)S(1)}, f32[16,128]{1,0:T(8,128)S(1)}, u32[]{:S(2)}, u32[]{:S(2)}) collective-permute-start(f32[16,128]{1,0:T(8,128)S(1)} %get-tuple-element.24), channel_id=1, source_target_pairs={{3,6},{7,10},{11,14},{15,18},{19,22},{23,26},{27,30}} | collective-permute-start | bytes 24584 | tf_op jit(solution)/shard_map/ppermute | solution.py:403
  41.0 1.8 %collective-permute-start.9 = (f32[32,128]{1,0:T(8,128)S(1)}, f32[32,128]{1,0:T(8,128)S(1)}, u32[]{:S(2)}, u32[]{:S(2)}) collective-permute-start(f32[32,128]{1,0:T(8,128)S(1)} %get-tuple-element.27), channel_id=1, source_target_pairs={{0,1},{1,0},{2,3},{3,2},{4,5},{5,4},{6,7},{7,6},{8,9},{9,8},{10,11... | collective-permute-start | bytes 49160 | tf_op jit(solution)/shard_map/ppermute | solution.py:358
where the time goes:
time: 44 us; the launch traced here: 43.4 us
  starting transfers between devices  15.5 us (35%)
  Pallas kernels  10.3 us (23%)
  waiting for transfers between devices  9.28 us (21%)
  local copies, waits for them, and re-layouts  6.89 us (16%)
  between operations  1.38 us (3%)
    pallas_call x6, Pallas kernels, run(): pl.pallas_call(kernel, out_shape=out_shape, in_specs=specs or [VMEM] * le...  10.3 us
    unnamed x20, local copies, waits for them, and re-layouts  6.89 us
    ppermute x4, starting transfers between devices, swap_sub(): return lax.ppermute(x, 'sub', [(i, i ^ mask) for i in range(subs)])  4.14 us
    ppermute x1, starting transfers between devices, local(): lax.ppermute(m1, AX, [p for i in range(1, total - 1, 2) for p in ((i, i +...  3.73 us
    ppermute x1, starting transfers between devices, local(): lax.ppermute(edge_msg, AX, [p for a, b in edges for p in ((a, b), (b, a))])  3.73 us
    ppermute x1, waiting for transfers between devices, local(): lax.ppermute(m1, AX, [p for i in range(1, total - 1, 2) for p in ((i, i +...  3.28 us
    ppermute x1, waiting for transfers between devices, local(): low_b = lax.ppermute(held, AX, [(b, a) for a, b in edges])  2.2 us
    ppermute x4, waiting for transfers between devices, swap_sub(): return lax.ppermute(x, 'sub', [(i, i ^ mask) for i in range(subs)])  1.67 us
  transfers between devices with their start and end apart: 10, of which 7 were waited for; matrix products, arithmetic and copies ran while one was open for 0% of the time, Pallas kernels for 0%

commit v1 on v0

--- a/solution.py
+++ b/solution.py
@@ -9,9 +9,11 @@
 
 BAND = 128
 LANE = 128
+WIDE = 256
 AX = ("curve", "sub")
 VMEM = pl.BlockSpec(memory_space=pltpu.VMEM)
 SMEM = pl.BlockSpec(memory_space=pltpu.SMEM)
+HBM = pl.BlockSpec(memory_space=pltpu.HBM)
 f32 = jnp.float32
 
 
@@ -28,15 +30,64 @@
     return order, masks
 
 
-def chain_mask(step, masks):
-    return masks[step]
-
-
-def pack_kernel(direction, velocity, owner, out):
-    out[0:8, :] = direction[...]
-    out[8:11, :] = velocity[:, :BAND]
-    out[11:12, :] = owner[:, :BAND].astype(f32)
+def fill(rest):
+    rest, pairs = list(rest), []
+    if len(rest) % 2:
+        a, b, c = rest[-3:]
+        rest = rest[:-3]
+        pairs += [(a, b), (b, c), (c, a)]
+    for i in range(0, len(rest), 2):
+        pairs += [(rest[i], rest[i + 1]), (rest[i + 1], rest[i])]
+    return pairs
+
+
+def edge_pairs(curves, subs, place):
+    pairs = []
+    for g in range(curves):
+        busy = set()
+        if g > 0:
+            busy.add(place)
+        if g < curves - 1:
+            busy.add(subs - 1)
+            a, b = subs * g + subs - 1, subs * (g + 1) + place
+            pairs += [(a, b), (b, a)]
+        pairs += fill(subs * g + i for i in range(subs) if i not in busy)
+    return pairs
+
+
+def pack_kernel(direction, velocity, owner, out, velocity_out, owner_out, dirs, sems):
+    copies = [
+        pltpu.make_async_copy(direction, dirs, sems.at[0]),
+        pltpu.make_async_copy(velocity, velocity_out, sems.at[1]),
+        pltpu.make_async_copy(owner, owner_out, sems.at[2]),
+    ]
+    for c in copies:
+        c.start()
+    for c in copies:
+        c.wait()
+    out[0:8, :] = dirs[...]
+    out[8:11, :] = velocity_out[:, :BAND]
+    out[11:12, :] = owner_out[:, :BAND].astype(f32)
     out[12:16, :] = jnp.zeros((4, LANE), f32)
+
+
+def prep_kernel(cfg, after, kmat, conn, weight, kmat_out, conn_out, weight_out, one_out, sems):
+    subs, order, masks, nodes, basal, corners = cfg
+    copies = [
+        pltpu.make_async_copy(conn, conn_out, sems.at[0]),
+        pltpu.make_async_copy(weight, weight_out, sems.at[1]),
+        pltpu.make_async_copy(kmat, kmat_out, sems.at[2]),
+    ]
+    for c in copies:
+        c.start()
+    copies[0].wait()
+    sub = lax.broadcasted_iota(jnp.int32, (WIDE, LANE), 0)
+    for n in range(corners):
+        row = conn_out[n : n + 1, :] - (nodes - BAND)
+        low = jnp.broadcast_to(row & (WIDE - 1), (WIDE, LANE))
+        one_out[:, n * LANE : (n + 1) * LANE] = (low == sub).astype(f32).astype(jnp.bfloat16)
+    copies[1].wait()
+    copies[2].wait()
 
 
 def grow_kernel(held, got, out):
@@ -77,21 +128,34 @@
             v_ref[c * corners + n] = acc
 
 
-def product(k_ref, v_ref, o_ref, count, size, group=9):
-    live = (lax.broadcasted_iota(jnp.int32, (8, LANE), 1) < count).astype(f32)
-
-    def step(i, carry):
-        start = i * group
+def product(k_ref, v_ref, o_ref, size, group=9):
+    count = size // group
+    for i in range(size):
+        o_ref[i] = jnp.zeros((8, LANE), f32)
+
+    def step(block, carry):
+        i0 = block * group
+        vi = [v_ref[i0 + t] for t in range(group)]
         acc = [jnp.zeros((8, LANE), f32) for _ in range(group)]
-        for j in range(size):
-            vj = v_ref[j]
+        for t in range(group):
+            for u in range(group):
+                acc[t] = acc[t] + rows8(k_ref[i0 + t, pl.ds(i0 + u, 1), :]) * vi[u]
+        for d in range(1, count // 2 + 1):
+            j0 = jnp.where(block + d >= count, block + d - count, block + d) * group
+            vj = [v_ref[j0 + u] for u in range(group)]
+            far = [o_ref[j0 + u] for u in range(group)]
             for t in range(group):
-                acc[t] = acc[t] + rows8(k_ref[start + t, j : j + 1, :]) * vj
+                for u in range(group):
+                    k = rows8(k_ref[i0 + t, pl.ds(j0 + u, 1), :])
+                    acc[t] = acc[t] + k * vj[u]
+                    far[u] = far[u] + k * vi[t]
+            for u in range(group):
+                o_ref[j0 + u] = far[u]
         for t in range(group):
-            o_ref[start + t] = acc[t] * live
+            o_ref[i0 + t] += acc[t]
         return carry
 
-    lax.fori_loop(0, size // group, step, 0)
+    lax.fori_loop(0, count, step, 0)
 
 
 def halves(x):
@@ -99,39 +163,34 @@
     return high, x - high
 
 
-def scatter_corners(o_ref, conn, base, corners, blocks, a_ref, one_ref):
-    sub = lax.broadcasted_iota(jnp.int32, (LANE, LANE), 0)
+def scatter_corners(o_ref, count, conn, base, corners, blocks, a_ref, one_ref):
+    live = lax.broadcasted_iota(jnp.int32, (8, LANE), 1) < count
+    wides = blocks * LANE // WIDE
     for n in range(corners):
-        row = conn[n : n + 1, :] - base
-        low = jnp.broadcast_to(row & (LANE - 1), (LANE, LANE))
-        one_ref[:, n * LANE : (n + 1) * LANE] = (low == sub).astype(f32).astype(jnp.bfloat16)
-        high = rows8(row >> 7)
+        high = jnp.where(live, rows8((conn[n : n + 1, :] - base) >> 8), -1)
         parts = [halves(o_ref[c * corners + n]) for c in range(3)]
-        pieces = [p[0] for p in parts] + [p[1] for p in parts]
-        for b in range(blocks):
-            here = high == b
-            stack = jnp.concatenate([jnp.where(here, p, 0.0) for p in pieces], axis=0)
-            a_ref[b * 48 : (b + 1) * 48, n * LANE : (n + 1) * LANE] = stack.astype(jnp.bfloat16)
+        stack = jnp.concatenate([p[0] for p in parts] + [p[1] for p in parts], axis=0).astype(jnp.bfloat16)
+        for b in range(wides):
+            here = (high == b).astype(f32).astype(jnp.bfloat16)
+            a_ref[b * 48 : (b + 1) * 48, n * LANE : (n + 1) * LANE] = stack * jnp.concatenate([here] * 6, axis=0)
     res = lax.dot_general(
         a_ref[...], one_ref[...], (((1,), (1,)), ((), ())), preferred_element_type=f32
     )
-    return [res[b * 48 : b * 48 + 24] + res[b * 48 + 24 : b * 48 + 48] for b in range(blocks)]
-
-
-def pick(index, options):
-    out = options[-1][1]
-    for value, array in options[:-1]:
-        out = jnp.where(index == value, array, out)
-    return out
+    sums = []
+    for b in range(wides):
+        both = res[b * 48 : b * 48 + 24] + res[b * 48 + 24 : b * 48 + 48]
+        sums += [both[:, h * LANE : (h + 1) * LANE] for h in range(WIDE // LANE)]
+    return sums
 
 
 def forward_kernel(cfg, *refs):
     subs, order, masks, nodes, basal, corners = cfg
     steps = len(masks)
     held, got, (low_b, mid_b) = refs[0], refs[1 : 1 + steps], refs[1 + steps : 3 + steps]
-    velocity, owner, weight, kmat, conn, count = refs[3 + steps : 9 + steps]
-    ext, m0, m1, info_out = refs[9 + steps : 13 + steps]
-    v_ref, o_ref, a_ref, one_ref = refs[13 + steps :]
+    velocity, owner, weight, kmat, conn, one_ref, count = refs[3 + steps : 10 + steps]
+    ext, edge_out, info_out = refs[10 + steps : 13 + steps]
+    swaps_out = refs[13 + steps : 13 + 2 * steps]
+    v_ref, o_ref, a_ref = refs[13 + 2 * steps :]
     s = lax.axis_index("sub")
     half = subs // 2
     own_blocks = nodes // LANE
@@ -167,31 +226,43 @@
     live_blocks = [1 + b for b in range(basal // LANE)] + [blocks - 1]
     base = nodes - BAND
     gather_corners(lambda c, b: values[c, b], live_blocks, conn, base, corners, v_ref)
-    product(kmat, v_ref, o_ref, count[0], 3 * corners)
-    sums = scatter_corners(o_ref, conn, base, corners, blocks, a_ref, one_ref)
+    product(kmat, v_ref, o_ref, 3 * corners)
+    sums = scatter_corners(o_ref, count[0], conn, base, corners, blocks, a_ref, one_ref)
     for b in range(blocks):
         ext[:, b * LANE : (b + 1) * LANE] = sums[b]
-    even = (s & 1) == 0
-    before = jnp.concatenate([sums[0], sums[1]], axis=1)
-    after = jnp.concatenate([sums[blocks - 2], sums[blocks - 1]], axis=1)
-    m0[0:24, :] = jnp.where(even, after, before)
-    m1[0:24, :] = jnp.where(even, before, after)
     pad = jnp.zeros((5, LANE), f32)
     none = jnp.zeros((8, LANE), f32)
     w_low = jnp.concatenate([weight[:, 0:BAND], pad], axis=0)
     w_high = jnp.concatenate([weight[:, nodes - BAND : nodes], pad], axis=0)
-    before = jnp.concatenate([none, w_low], axis=1)
-    after = jnp.concatenate([w_high, none], axis=1)
-    m0[24:32, :] = jnp.where(even, after, before)
-    m1[24:32, :] = jnp.where(even, before, after)
+    before = ((sums[0], none), (sums[1], w_low))
+    after = ((sums[blocks - 2], w_high), (sums[blocks - 1], none))
+    for col in range(2):
+        for part, rows in ((0, slice(0, 24)), (1, slice(24, 32))):
+            down, up = before[col][part], after[col][part]
+            lanes = slice(col * LANE, (col + 1) * LANE)
+            for t in range(steps):
+                swaps_out[t][rows, lanes] = jnp.where((s & (1 << t)) == 0, up, down)
+            edge_out[rows, lanes] = jnp.where(last, up, jnp.where(s == 0, down, 0.0))
+
+
+def neighbours(s, edge, swaps, subs):
+    prev = nxt = edge
+    for t, got in enumerate(swaps):
+        ones = (1 << t) - 1
+        nxt = jnp.where((s & (2 * ones + 1)) == ones, got, nxt)
+        prev = jnp.where((s & (2 * ones + 1)) == ones + 1, got, prev)
+    nxt = jnp.where(s == subs - 1, edge, nxt)
+    return prev, nxt
 
 
 def adjoint_kernel(cfg, *refs):
     subs, order, masks, nodes, basal, corners = cfg
-    ext, r0, r1, info, velocity, owner, weight, kmat, conn, count = refs[:10]
-    n_out = 4 + len(masks)
-    outs = refs[10 : 10 + n_out]
-    v_ref, o_ref, a_ref, one_ref = refs[10 + n_out :]
+    steps = len(masks)
+    ext, edge_in, info, velocity, owner, weight, kmat, conn, one_ref, count = refs[:10]
+    swaps_in = refs[10 : 10 + steps]
+    n_out = 4 + steps
+    outs = refs[10 + steps : 10 + steps + n_out]
+    v_ref, o_ref, a_ref = refs[10 + steps + n_out :]
     own_out, swap_out, edge_out, mid_out = outs[:4]
     dense_out = outs[4]
     band_outs = outs[5:]
@@ -199,11 +270,8 @@
     half = subs // 2
     blocks = nodes // LANE + 2
     last = s == subs - 1
-    even = (s & 1) == 0
     base = nodes - BAND
-
-    prev = jnp.where(even, r1[...], r0[...])
-    nxt = jnp.where(even, r0[...], r1[...])
+    prev, nxt = neighbours(s, edge_in[...], [x[...] for x in swaps_in], subs)
 
     values = {}
     for c in range(3):
@@ -222,8 +290,8 @@
                 x = x * rows8(weight[c : c + 1, (b - 1) * LANE : b * LANE])
             values[c, b] = x
     gather_corners(lambda c, b: values[c, b], range(blocks), conn, base, corners, v_ref)
-    product(kmat, v_ref, o_ref, count[0], 3 * corners)
-    sums = scatter_corners(o_ref, conn, base, corners, blocks, a_ref, one_ref)
+    product(kmat, v_ref, o_ref, 3 * corners)
+    sums = scatter_corners(o_ref, count[0], conn, base, corners, blocks, a_ref, one_ref)
     for b in range(1, blocks - 1):
         own_out[:, (b - 1) * LANE : b * LANE] = sums[b]
     lower, upper = sums[0], sums[blocks - 1]
@@ -282,7 +350,7 @@
         swap_out[8 * q : 8 * q + 8, :] = dense[half + q]
         edge_out[8 * q : 8 * q + 8, :] = dense[subs + q]
         mid_out[8 * q : 8 * q + 8, :] = dense[subs + half + q]
-    edge_out[rows : rows + 24, :] = jnp.where(last, upper, lower)
+    edge_out[rows : rows + 24, :] = jnp.where(last, upper, jnp.where(s == 0, lower, 0.0))
     up = (s & half) == 0
     swap_out[rows : rows + 24, :] = jnp.where(up, upper, lower)
     for t, band in enumerate(band_outs):
@@ -314,12 +382,7 @@
     s = lax.axis_index("sub")
     gradient[...] = held[...] + got[0][0:8, :]
     bands = [g[g.shape[0] - 24 :, :] for g in got]
-    prev = edge[edge.shape[0] - 24 :, :]
-    nxt = prev
-    for t in range(steps):
-        ones = (1 << t) - 1
-        nxt = jnp.where((s & (2 * ones + 1)) == ones, bands[t], nxt)
-        prev = jnp.where((s & (2 * ones + 1)) == ones + 1, bands[t], prev)
+    prev, nxt = neighbours(s, edge[edge.shape[0] - 24 :, :], bands, subs)
     field[:, 0:LANE] = own[:, 0:LANE] + prev
     field[:, LANE : nodes - LANE] = own[:, LANE : nodes - LANE]
     field[:, nodes - LANE :] = own[:, nodes - LANE :] + nxt
@@ -331,7 +394,6 @@
 
 def local(curves, subs, direction, base_velocity, weight, element_matrix, connectivity, element_count, basal_owner):
     order, masks = xor_order(subs)
-    total = curves * subs
     half = subs // 2
     nodes = base_velocity.shape[1]
     basal = basal_owner.shape[0]
@@ -341,7 +403,7 @@
     cfg = (subs, order, masks, nodes, basal, corners)
     owner = basal_owner.reshape(1, basal)
 
-    def call(kernel, out_shape, scratch=(), mib=4, specs=None):
+    def call(kernel, out_shape, scratch=(), mib=4, specs=None, cost=None):
         def run(*args):
             return pl.pallas_call(
                 kernel,
@@ -350,6 +412,7 @@
                 out_specs=jax.tree.map(lambda _: VMEM, out_shape),
                 scratch_shapes=list(scratch),
                 compiler_params=params(mib),
+                cost_estimate=cost,
             )(*args)
 
         return run
@@ -357,50 +420,69 @@
     def swap_sub(x, mask):
         return lax.ppermute(x, "sub", [(i, i ^ mask) for i in range(subs)])
 
-    edges = [(subs * g + subs - 1, subs * (g + 1)) for g in range(curves - 1)]
-
-    held = call(pack_kernel, shape(16, LANE))(direction, base_velocity, owner)
+    def swap_edge(x, place):
+        return lax.ppermute(x, AX, edge_pairs(curves, subs, place))
+
+    steps = len(masks)
+    rows = 8 * half
+
+    held, velocity, owner = call(
+        pack_kernel,
+        (shape(16, LANE), shape(3, nodes), jax.ShapeDtypeStruct((1, basal), jnp.int32)),
+        [pltpu.VMEM((8, LANE), f32), pltpu.SemaphoreType.DMA((3,))],
+        specs=[HBM] * 3,
+    )(direction, base_velocity, owner)
     got = []
     for mask in masks[:-1]:
         got.append(swap_sub(held, mask))
-        rows = 2 * held.shape[0] - 8
-        held = call(grow_kernel, shape(rows, LANE))(held, got[-1])
+        held = call(grow_kernel, shape(2 * held.shape[0] - 8, LANE))(held, got[-1])
+    low_b = swap_edge(held, 0)
+    mid_b = swap_edge(held, half)
     got.append(swap_sub(held, masks[-1]))
-    low_b = lax.ppermute(held, AX, [(b, a) for a, b in edges])
-    mid_b = lax.ppermute(held, AX, [(b + half, a) for a, b in edges])
+
+    kmat, conn, weight, one = call(
+        functools.partial(prep_kernel, cfg),
+        (
+            shape(size, size, elems),
+            jax.ShapeDtypeStruct((corners, elems), jnp.int32),
+            shape(3, nodes),
+            jax.ShapeDtypeStruct((WIDE, corners * LANE), jnp.bfloat16),
+        ),
+        [pltpu.SemaphoreType.DMA((3,))],
+        16,
+        [VMEM] + [HBM] * 3,
+        pl.CostEstimate(flops=0, bytes_accessed=8 << 20, transcendentals=0),
+    )(held, element_matrix, connectivity, weight)
 
     scratch = [
         pltpu.VMEM((size, 8, LANE), f32),
         pltpu.VMEM((size, 8, LANE), f32),
-        pltpu.VMEM((48 * blocks, corners * LANE), jnp.bfloat16),
-        pltpu.VMEM((LANE, corners * LANE), jnp.bfloat16),
+        pltpu.VMEM((48 * blocks * LANE // WIDE, corners * LANE), jnp.bfloat16),
     ]
-    ext, m0, m1, info = call(
+    ext, edge, info, *swaps = call(
         functools.partial(forward_kernel, cfg),
-        (shape(24, blocks * LANE), shape(32, 2 * LANE), shape(32, 2 * LANE), shape(8, LANE)),
+        (shape(24, blocks * LANE), shape(32, 2 * LANE), shape(8, LANE)) + (shape(32, 2 * LANE),) * steps,
         scratch,
         16,
-        [VMEM] * (8 + len(got)) + [SMEM],
-    )(held, *got, low_b, mid_b, base_velocity, owner, weight, element_matrix, connectivity, element_count)
-
-    r0 = lax.ppermute(m0, AX, [p for i in range(0, total - 1, 2) for p in ((i, i + 1), (i + 1, i))])
-    r1 = lax.ppermute(m1, AX, [p for i in range(1, total - 1, 2) for p in ((i, i + 1), (i + 1, i))])
-
-    steps = len(masks)
-    rows = 8 * half
+        [VMEM] * (9 + steps) + [SMEM],
+    )(held, *got, low_b, mid_b, velocity, owner, weight, kmat, conn, one, element_count)
+
+    edge = swap_edge(edge, 0)
+    swaps = [swap_sub(x, mask) for x, mask in zip(swaps, masks)]
+
     own, swap_msg, edge_msg, mid_msg, dense, *bands = call(
         functools.partial(adjoint_kernel, cfg),
         (shape(24, nodes), shape(rows + 24, LANE), shape(rows + 24, LANE), shape(rows, LANE), shape(rows, LANE))
         + (shape(24, LANE),) * (steps - 1),
         scratch,
         16,
-        [VMEM] * 9 + [SMEM],
-    )(ext, r0, r1, info, base_velocity, owner, weight, element_matrix, connectivity, element_count)
-
+        [VMEM] * 9 + [SMEM] + [VMEM] * steps,
+    )(ext, edge, info, velocity, owner, weight, kmat, conn, one, element_count, *swaps)
+
+    edge = swap_edge(edge_msg, 0)
+    mid = swap_edge(mid_msg, half)
     by_mask = [None] * steps
     by_mask[-1] = swap_sub(swap_msg, masks[-1])
-    edge = lax.ppermute(edge_msg, AX, [p for a, b in edges for p in ((a, b), (b, a))])
-    mid = lax.ppermute(mid_msg, AX, [(a, b + half) for a, b in edges])
     extra = (edge, mid)
     for t in range(steps - 2, -1, -1):
         keep = dense.shape[0] // 2

time: 44 us -> 33.3 us (0.76)
  starting transfers between devices: 15.5 us -> 8.87 us
  Pallas kernels: 10.3 us -> 8.01 us
  local copies, waits for them, and re-layouts: 6.89 us -> 5.5 us
    ppermute x6 -> x5, starting transfers between devices: 11.4 us -> 5.62 us  [swap_edge(): return lax.ppermute(x, AX, edge_pairs(curves, subs, place))]
    pallas_call x6 -> x7, Pallas kernels: 10.3 us -> 8.01 us  [run(): pl.pallas_call(kernel, out_shape=out_shape, in_specs=specs or [VMEM] * le...]
    unnamed x20 -> x12, local copies, waits for them, and re-layouts: 6.89 us -> 5.5 us
    ppermute x6 -> x5, waiting for transfers between devices: 7.61 us -> 6.45 us  [swap_edge(): return lax.ppermute(x, AX, edge_pairs(curves, subs, place))]
    ppermute x4 -> x6, waiting for transfers between devices: 1.67 us -> 2.63 us  [swap_sub(): return lax.ppermute(x, 'sub', [(i, i ^ mask) for i in range(subs)])]
    ppermute x4 -> x6, starting transfers between devices: 4.14 us -> 3.25 us  [swap_sub(): return lax.ppermute(x, 'sub', [(i, i ^ mask) for i in range(subs)])]
  transfers between devices with their start and end apart: 10 -> 11, of which waited for: 7 -> 5; matrix products, arithmetic and copies ran while one was open for 0% -> 0% of each run, Pallas kernels for 0% -> 2%
where the time goes in v1:
time: 33.3 us; the launch traced here: 32.8 us
  waiting for transfers between devices  9.09 us (27%)
  starting transfers between devices  8.87 us (27%)
  Pallas kernels  8.01 us (24%)
  local copies, waits for them, and re-layouts  5.5 us (17%)
  between operations  1.38 us (4%)
    pallas_call x7, Pallas kernels, run(): pl.pallas_call(kernel, out_shape=out_shape, in_specs=specs or [VMEM] * le...  8.01 us
    ppermute x5, waiting for transfers between devices, swap_edge(): return lax.ppermute(x, AX, edge_pairs(curves, subs, place))  6.45 us
    ppermute x5, starting transfers between devices, swap_edge(): return lax.ppermute(x, AX, edge_pairs(curves, subs, place))  5.62 us
    unnamed x12, local copies, waits for them, and re-layouts  5.5 us
    ppermute x6, starting transfers between devices, swap_sub(): return lax.ppermute(x, 'sub', [(i, i ^ mask) for i in range(subs)])  3.25 us
    ppermute x6, waiting for transfers between devices, swap_sub(): return lax.ppermute(x, 'sub', [(i, i ^ mask) for i in range(subs)])  2.63 us
  transfers between devices with their start and end apart: 11, of which 5 were waited for; matrix products, arithmetic and copies ran while one was open for 0% of the time, Pallas kernels for 2%

profile of v1, /device:TPU:15, one launch (start us, length us, event | category | flops | bytes accessed | tf_op | source)
XLA Modules:
  0.0 32.8 jit_solution(7232076947776338248)
XLA Ops:
  0.6 0.0 copy-start.3
  0.6 0.7 %copy-done.3 = f32[3,512]{1,0:T(4,128)S(1)} copy-done((f32[3,512]{1,0:T(4,128)S(1)}, f32[3,512]{1,0:T(4,128)}, u32[]{:S(2)}) %copy-start.3) | copy-done | bytes 6168
  1.3 0.0 copy-start.4
  1.3 0.7 %copy-done.4 = f32[8,128]{1,0:T(8,128)S(1)} copy-done((f32[8,128]{1,0:T(8,128)S(1)}, f32[8,128]{1,0:T(8,128)}, u32[]{:S(2)}) %copy-start.4) | copy-done | bytes 4120
  2.0 0.0 copy-start.5
  2.0 0.7 %copy-done.5 = s32[256]{0:T(256)S(1)} copy-done((s32[256]{0:T(256)S(1)}, s32[256]{0:T(256)}, u32[]{:S(2)}) %copy-start.5) | copy-done | bytes 1048
  2.7 0.7 %collective-permute-start = (f32[16,128]{1,0:T(8,128)S(1)}, f32[16,128]{1,0:T(8,128)S(1)}, u32[]{:S(2)}, u32[]{:S(2)}) collective-permute-start(f32[16,128]{1,0:T(8,128)S(1)} %get-tuple-element.24.held), channel_id=1, source_target_pairs={{0,1},{1,0},{2,3},{3,2},{4,5},{5,4},{6,7},{7,6},{8,9},{9,8},{10,11... | collective-permute-start | bytes 24584 | tf_op jit(solution)/shard_map/ppermute | solution.py:421
  3.5 0.8 %collective-permute-done.got.refs_1_ = f32[16,128]{1,0:T(8,128)S(1)} collective-permute-done((f32[16,128]{1,0:T(8,128)S(1)}, f32[16,128]{1,0:T(8,128)S(1)}, u32[]{:S(2)}, u32[]{:S(2)}) %collective-permute-start) | collective-permute-done | bytes 8224 | tf_op jit(solution)/shard_map/ppermute | solution.py:421
  4.3 1.5 %collective-permute-start.3 = (f32[24,128]{1,0:T(8,128)S(1)}, f32[24,128]{1,0:T(8,128)S(1)}, u32[]{:S(2)}, u32[]{:S(2)}) collective-permute-start(f32[24,128]{1,0:T(8,128)S(1)} %shard_map.87.after.refs_0_), channel_id=1, source_target_pairs={{3,6},{6,3},{0,1},{1,2},{2,0},{7,10},{10,7},{4,5},{5,4},{11,14},{1... | collective-permute-start | bytes 36872 | tf_op jit(solution)/shard_map/ppermute | solution.py:424
  5.8 0.1 collective-permute-start.2
  5.9 1.6 %collective-permute-start.1 = (f32[24,128]{1,0:T(8,128)S(1)}, f32[24,128]{1,0:T(8,128)S(1)}, u32[]{:S(2)}, u32[]{:S(2)}) collective-permute-start(f32[24,128]{1,0:T(8,128)S(1)} %shard_map.87.after.refs_0_), channel_id=1, source_target_pairs={{0,3},{1,2},{2,1},{3,0},{4,7},{5,6},{6,5},{7,4},{8,11},{9,10},{10,... | collective-permute-start | bytes 36872 | tf_op jit(solution)/shard_map/ppermute | solution.py:421
  8.1 0.0 copy-start
  8.1 2.0 %copy-done = f32[81,81,128]{2,1,0:T(8,128)S(1)} copy-done((f32[81,81,128]{2,1,0:T(8,128)S(1)}, f32[81,81,128]{2,1,0:T(8,128)}, u32[]{:S(2)}) %copy-start) | copy-done | bytes 3359256
  10.2 0.0 copy-start.1
  10.2 0.7 %copy-done.1 = s32[27,128]{1,0:T(8,128)S(1)} copy-done((s32[27,128]{1,0:T(8,128)S(1)}, s32[27,128]{1,0:T(8,128)}, u32[]{:S(2)}) %copy-start.1) | copy-done | bytes 13848
  10.9 0.0 copy-start.2
  10.9 0.7 %copy-done.2 = f32[3,512]{1,0:T(4,128)S(1)} copy-done((f32[3,512]{1,0:T(4,128)S(1)}, f32[3,512]{1,0:T(4,128)}, u32[]{:S(2)}) %copy-start.2) | copy-done | bytes 6168
  11.6 0.7 %shard_map.88 = (f32[81,81,128]{2,1,0:T(8,128)S(1)}, s32[27,128]{1,0:T(8,128)S(1)}, f32[3,512]{1,0:T(4,128)S(1)}, bf16[256,3456]{1,0:T(8,128)(2,1)S(1)}) custom-call(f32[24,128]{1,0:T(8,128)S(1)} %shard_map.87.after.refs_0_, f32[81,81,128]{2,1,0:T(8,128)S(1)} %copy-done, s32[27,128]{1,0:T(8,128)S(1)} %copy-done.1, f32[3,512]{1,0:T(4,128)S(1)} %copy-done.2), custom_call_target="tpu_custom_call" | custom-call | bytes 8388608 | tf_op jit(solution)/shard_map/pallas_call | solution.py:408
  12.2 0.0 collective-permute-done.3.refs_4_
  12.2 0.0 collective-permute-done.2.refs_3_
  12.3 0.0 collective-permute-done.1.refs_2_
  12.3 3.2 %shard_map.89 = (f32[24,768]{1,0:T(8,128)S(1)}, f32[32,256]{1,0:T(8,128)S(1)}, f32[8,128]{1,0:T(8,128)S(1)}, f32[32,256]{1,0:T(8,128)S(1)}, f32[32,256]{1,0:T(8,128)S(1)}) custom-call(f32[24,128]{1,0:T(8,128)S(1)} %shard_map.87.after.refs_0_, f32[16,128]{1,0:T(8,128)S(1)} %collective-permute-done.got.refs_1_, f32[24,128]{1,0:T(8,128)S(1)} %collective-permute-done.1.refs_2_, ...), custom_call_target="tpu_custom_call" | custom-call | tf_op jit(solution)/shard_map/pallas_call | solution.py:408
  15.4 1.9 %collective-permute-start.4 = (f32[32,256]{1,0:T(8,128)S(1)}, f32[32,256]{1,0:T(8,128)S(1)}, u32[]{:S(2)}, u32[]{:S(2)}) collective-permute-start(f32[32,256]{1,0:T(8,128)S(1)} %get-tuple-element.32), channel_id=1, source_target_pairs={{3,4},{4,3},{0,1},{1,2},{2,0},{7,8},{8,7},{5,6},{6,5},{11,12},{12,... | collective-permute-start | bytes 98312 | tf_op jit(solution)/shard_map/ppermute | solution.py:424
  17.4 0.0 collective-permute-start.5
  17.4 0.7 %collective-permute-start.6 = (f32[32,256]{1,0:T(8,128)S(1)}, f32[32,256]{1,0:T(8,128)S(1)}, u32[]{:S(2)}, u32[]{:S(2)}) collective-permute-start(f32[32,256]{1,0:T(8,128)S(1)} %get-tuple-element.35), channel_id=1, source_target_pairs={{0,3},{1,2},{2,1},{3,0},{4,7},{5,6},{6,5},{7,4},{8,11},{9,10},{10,... | collective-permute-start | bytes 98312 | tf_op jit(solution)/shard_map/ppermute | solution.py:421
  18.1 2.6 %collective-permute-done.4.refs_1_ = f32[32,256]{1,0:T(8,128)S(1)} collective-permute-done((f32[32,256]{1,0:T(8,128)S(1)}, f32[32,256]{1,0:T(8,128)S(1)}, u32[]{:S(2)}, u32[]{:S(2)}) %collective-permute-start.4) | collective-permute-done | bytes 32800 | tf_op jit(solution)/shard_map/ppermute | solution.py:424
  20.7 0.0 collective-permute-done.5.refs_10_
  20.7 0.6 %collective-permute-done.6.refs_11_ = f32[32,256]{1,0:T(8,128)S(1)} collective-permute-done((f32[32,256]{1,0:T(8,128)S(1)}, f32[32,256]{1,0:T(8,128)S(1)}, u32[]{:S(2)}, u32[]{:S(2)}) %collective-permute-start.6) | collective-permute-done | bytes 32800 | tf_op jit(solution)/shard_map/ppermute | solution.py:421
  21.4 3.5 %shard_map.90 = (f32[24,512]{1,0:T(8,128)S(1)}, f32[40,128]{1,0:T(8,128)S(1)}, f32[40,128]{1,0:T(8,128)S(1)}, f32[16,128]{1,0:T(8,128)S(1)}, f32[16,128]{1,0:T(8,128)S(1)}, /*index=5*/f32[24,128]{1,0:T(8,128)S(1)}) custom-call(f32[24,768]{1,0:T(8,128)S(1)} %get-tuple-element.31.refs_0_, f32[32,256]{1,0:T(8,128)S(1)} %collective-permute-done.4.refs_1_, ...), custom_call_target="tpu_custom_call" | custom-call | tf_op jit(solution)/shard_map/pallas_call | solution.py:408
  24.9 0.2 collective-permute-start.7
  25.0 1.9 %collective-permute-start.8 = (f32[40,128]{1,0:T(8,128)S(1)}, f32[40,128]{1,0:T(8,128)S(1)}, u32[]{:S(2)}, u32[]{:S(2)}) collective-permute-start(f32[40,128]{1,0:T(8,128)S(1)} %get-tuple-element.39), channel_id=1, source_target_pairs={{3,4},{4,3},{0,1},{1,2},{2,0},{7,8},{8,7},{5,6},{6,5},{11,12},{12,... | collective-permute-start | bytes 61448 | tf_op jit(solution)/shard_map/ppermute | solution.py:424
  27.0 0.2 collective-permute-start.9
  27.1 3.8 %collective-permute-done.9.refs_3_ = f32[16,128]{1,0:T(8,128)S(1)} collective-permute-done((f32[16,128]{1,0:T(8,128)S(1)}, f32[16,128]{1,0:T(8,128)S(1)}, u32[]{:S(2)}, u32[]{:S(2)}) %collective-permute-start.9) | collective-permute-done | bytes 8224 | tf_op jit(solution)/shard_map/ppermute | solution.py:424
  30.9 0.0 collective-permute-done.7.refs_1_.refs_4_
  30.9 0.0 collective-permute-done.8.refs_2_
  30.9 0.1 collective-permute-start.10
  31.0 1.2 %collective-permute-done.10.refs_3_ = f32[32,128]{1,0:T(8,128)S(1)} collective-permute-done((f32[32,128]{1,0:T(8,128)S(1)}, f32[32,128]{1,0:T(8,128)S(1)}, u32[]{:S(2)}, u32[]{:S(2)}) %collective-permute-start.10) | collective-permute-done | bytes 16416 | tf_op jit(solution)/shard_map/ppermute | solution.py:421
  32.2 0.6 %shard_map.92 = (f32[8,128]{1,0:T(8,128)}, f32[24,512]{1,0:T(8,128)}) custom-call(f32[24,512]{1,0:T(8,128)S(1)} %get-tuple-element.36.refs_0_, f32[8,128]{1,0:T(8,128)S(1)} %get-tuple-element.42.refs_1_, f32[40,128]{1,0:T(8,128)S(1)} %collective-permute-done.8.refs_2_, f32[32,128]{1,0:T(8,128)S(1)} %collective-permute-done.10.refs_3_, ...), custom_call_target="tpu_custom_call" | custom-call | tf_op jit(solution)/shard_map/pallas_call | solution.py:408
  (3 shorter events, 0.0 us)
Async XLA Ops:
  0.6 0.7 %copy-start.3 = (f32[3,512]{1,0:T(4,128)S(1)}, f32[3,512]{1,0:T(4,128)}, u32[]{:S(2)}) copy-start(f32[3,512]{1,0:T(4,128)} %velocity.1) | copy-start | bytes 18436
  1.3 0.7 %copy-start.4 = (f32[8,128]{1,0:T(8,128)S(1)}, f32[8,128]{1,0:T(8,128)}, u32[]{:S(2)}) copy-start(f32[8,128]{1,0:T(8,128)} %direction.1) | copy-start | bytes 12292
  2.0 0.7 %copy-start.5 = (s32[256]{0:T(256)S(1)}, s32[256]{0:T(256)}, u32[]{:S(2)}) copy-start(s32[256]{0:T(256)} %param.13) | copy-start | bytes 3076
  2.7 1.6 %collective-permute-start = (f32[16,128]{1,0:T(8,128)S(1)}, f32[16,128]{1,0:T(8,128)S(1)}, u32[]{:S(2)}, u32[]{:S(2)}) collective-permute-start(f32[16,128]{1,0:T(8,128)S(1)} %get-tuple-element.24.held), channel_id=1, source_target_pairs={{0,1},{1,0},{2,3},{3,2},{4,5},{5,4},{6,7},{7,6},{8,9},{9,8},{10,11... | collective-permute-start | bytes 24584 | tf_op jit(solution)/shard_map/ppermute | solution.py:421
  4.3 7.9 %collective-permute-start.3 = (f32[24,128]{1,0:T(8,128)S(1)}, f32[24,128]{1,0:T(8,128)S(1)}, u32[]{:S(2)}, u32[]{:S(2)}) collective-permute-start(f32[24,128]{1,0:T(8,128)S(1)} %shard_map.87.after.refs_0_), channel_id=1, source_target_pairs={{3,6},{6,3},{0,1},{1,2},{2,0},{7,10},{10,7},{4,5},{5,4},{11,14},{1... | collective-permute-start | bytes 36872 | tf_op jit(solution)/shard_map/ppermute | solution.py:424
  5.8 6.4 %collective-permute-start.2 = (f32[24,128]{1,0:T(8,128)S(1)}, f32[24,128]{1,0:T(8,128)S(1)}, u32[]{:S(2)}, u32[]{:S(2)}) collective-permute-start(f32[24,128]{1,0:T(8,128)S(1)} %shard_map.87.after.refs_0_), channel_id=1, source_target_pairs={{3,4},{4,3},{0,1},{1,2},{2,0},{7,8},{8,7},{5,6},{6,5},{11,12},{12,... | collective-permute-start | bytes 36872 | tf_op jit(solution)/shard_map/ppermute | solution.py:424
  5.9 6.3 %collective-permute-start.1 = (f32[24,128]{1,0:T(8,128)S(1)}, f32[24,128]{1,0:T(8,128)S(1)}, u32[]{:S(2)}, u32[]{:S(2)}) collective-permute-start(f32[24,128]{1,0:T(8,128)S(1)} %shard_map.87.after.refs_0_), channel_id=1, source_target_pairs={{0,3},{1,2},{2,1},{3,0},{4,7},{5,6},{6,5},{7,4},{8,11},{9,10},{10,... | collective-permute-start | bytes 36872 | tf_op jit(solution)/shard_map/ppermute | solution.py:421
  8.1 2.0 %copy-start = (f32[81,81,128]{2,1,0:T(8,128)S(1)}, f32[81,81,128]{2,1,0:T(8,128)}, u32[]{:S(2)}) copy-start(f32[81,81,128]{2,1,0:T(8,128)} %kmat.1) | copy-start | bytes 10077700
  10.2 0.7 %copy-start.1 = (s32[27,128]{1,0:T(8,128)S(1)}, s32[27,128]{1,0:T(8,128)}, u32[]{:S(2)}) copy-start(s32[27,128]{1,0:T(8,128)} %conn.1) | copy-start | bytes 41476
  10.9 0.7 %copy-start.2 = (f32[3,512]{1,0:T(4,128)S(1)}, f32[3,512]{1,0:T(4,128)}, u32[]{:S(2)}) copy-start(f32[3,512]{1,0:T(4,128)} %weight.1) | copy-start | bytes 18436
  15.4 5.3 %collective-permute-start.4 = (f32[32,256]{1,0:T(8,128)S(1)}, f32[32,256]{1,0:T(8,128)S(1)}, u32[]{:S(2)}, u32[]{:S(2)}) collective-permute-start(f32[32,256]{1,0:T(8,128)S(1)} %get-tuple-element.32), channel_id=1, source_target_pairs={{3,4},{4,3},{0,1},{1,2},{2,0},{7,8},{8,7},{5,6},{6,5},{11,12},{12,... | collective-permute-start | bytes 98312 | tf_op jit(solution)/shard_map/ppermute | solution.py:424
  17.4 3.4 %collective-permute-start.5 = (f32[32,256]{1,0:T(8,128)S(1)}, f32[32,256]{1,0:T(8,128)S(1)}, u32[]{:S(2)}, u32[]{:S(2)}) collective-permute-start(f32[32,256]{1,0:T(8,128)S(1)} %get-tuple-element.34), channel_id=1, source_target_pairs={{0,1},{1,0},{2,3},{3,2},{4,5},{5,4},{6,7},{7,6},{8,9},{9,8},{10,11... | collective-permute-start | bytes 98312 | tf_op jit(solution)/shard_map/ppermute | solution.py:421
  17.4 4.0 %collective-permute-start.6 = (f32[32,256]{1,0:T(8,128)S(1)}, f32[32,256]{1,0:T(8,128)S(1)}, u32[]{:S(2)}, u32[]{:S(2)}) collective-permute-start(f32[32,256]{1,0:T(8,128)S(1)} %get-tuple-element.35), channel_id=1, source_target_pairs={{0,3},{1,2},{2,1},{3,0},{4,7},{5,6},{6,5},{7,4},{8,11},{9,10},{10,... | collective-permute-start | bytes 98312 | tf_op jit(solution)/shard_map/ppermute | solution.py:421
  24.9 6.1 %collective-permute-start.7 = (f32[40,128]{1,0:T(8,128)S(1)}, f32[40,128]{1,0:T(8,128)S(1)}, u32[]{:S(2)}, u32[]{:S(2)}) collective-permute-start(f32[40,128]{1,0:T(8,128)S(1)} %get-tuple-element.38), channel_id=1, source_target_pairs={{0,3},{1,2},{2,1},{3,0},{4,7},{5,6},{6,5},{7,4},{8,11},{9,10},{10,... | collective-permute-start | bytes 61448 | tf_op jit(solution)/shard_map/ppermute | solution.py:421
  25.0 5.9 %collective-permute-start.8 = (f32[40,128]{1,0:T(8,128)S(1)}, f32[40,128]{1,0:T(8,128)S(1)}, u32[]{:S(2)}, u32[]{:S(2)}) collective-permute-start(f32[40,128]{1,0:T(8,128)S(1)} %get-tuple-element.39), channel_id=1, source_target_pairs={{3,4},{4,3},{0,1},{1,2},{2,0},{7,8},{8,7},{5,6},{6,5},{11,12},{12,... | collective-permute-start | bytes 61448 | tf_op jit(solution)/shard_map/ppermute | solution.py:424
  27.0 4.0 %collective-permute-start.9 = (f32[16,128]{1,0:T(8,128)S(1)}, f32[16,128]{1,0:T(8,128)S(1)}, u32[]{:S(2)}, u32[]{:S(2)}) collective-permute-start(f32[16,128]{1,0:T(8,128)S(1)} %get-tuple-element.40), channel_id=1, source_target_pairs={{3,6},{6,3},{0,1},{1,2},{2,0},{7,10},{10,7},{4,5},{5,4},{11,14},{1... | collective-permute-start | bytes 24584 | tf_op jit(solution)/shard_map/ppermute | solution.py:424
  30.9 1.2 %collective-permute-start.10 = (f32[32,128]{1,0:T(8,128)S(1)}, f32[32,128]{1,0:T(8,128)S(1)}, u32[]{:S(2)}, u32[]{:S(2)}) collective-permute-start(f32[32,128]{1,0:T(8,128)S(1)} %get-tuple-element.43), channel_id=1, source_target_pairs={{0,1},{1,0},{2,3},{3,2},{4,5},{5,4},{6,7},{7,6},{8,9},{9,8},{10,11... | collective-permute-start | bytes 49160 | tf_op jit(solution)/shard_map/ppermute | solution.py:421

commit v2 on v1

--- a/solution.py
+++ b/solution.py
@@ -405,6 +405,10 @@
 
     def call(kernel, out_shape, scratch=(), mib=4, specs=None, cost=None):
         def run(*args):
+            args = [
+                pltpu.with_memory_space_constraint(x, pltpu.HBM) if specs and specs[i] is HBM else x
+                for i, x in enumerate(args)
+            ]
             return pl.pallas_call(
                 kernel,
                 out_shape=out_shape,

time: 33.3 us -> 29.8 us (0.89)
  local copies, waits for them, and re-layouts: 5.5 us -> 0 us
  Pallas kernels: 8.01 us -> 10 us
  waiting for transfers between devices: 9.09 us -> 9.89 us
  starting transfers between devices: 8.87 us -> 8.16 us
    unnamed x12 -> x0, local copies, waits for them, and re-layouts: 5.5 us -> none
    pallas_call x7, Pallas kernels: 8.01 us -> 10 us  [run(): pl.pallas_call(kernel, out_shape=out_shape, in_specs=specs or [VMEM] * le...]
    ppermute x5, waiting for transfers between devices: 6.45 us -> 7.42 us  [swap_edge(): return lax.ppermute(x, AX, edge_pairs(curves, subs, place))]
    ppermute x6, starting transfers between devices: 3.25 us -> 2.76 us  [swap_sub(): return lax.ppermute(x, 'sub', [(i, i ^ mask) for i in range(subs)])]
  transfers between devices with their start and end apart: 11 -> 11, of which waited for: 5 -> 6; matrix products, arithmetic and copies ran while one was open for 0% -> 0% of each run, Pallas kernels for 2% -> 7%
where the time goes in v2:
time: 29.8 us; the launch traced here: 29.4 us
  Pallas kernels  10 us (34%)
  waiting for transfers between devices  9.89 us (33%)
  starting transfers between devices  8.16 us (27%)
  between operations  1.35 us (5%)
    pallas_call x7, Pallas kernels, run(): pl.pallas_call(kernel, out_shape=out_shape, in_specs=specs or [VMEM] * le...  10 us
    ppermute x5, waiting for transfers between devices, swap_edge(): return lax.ppermute(x, AX, edge_pairs(curves, subs, place))  7.42 us
    ppermute x5, starting transfers between devices, swap_edge(): return lax.ppermute(x, AX, edge_pairs(curves, subs, place))  5.4 us
    ppermute x6, starting transfers between devices, swap_sub(): return lax.ppermute(x, 'sub', [(i, i ^ mask) for i in range(subs)])  2.76 us
    ppermute x6, waiting for transfers between devices, swap_sub(): return lax.ppermute(x, 'sub', [(i, i ^ mask) for i in range(subs)])  2.47 us
  transfers between devices with their start and end apart: 11, of which 6 were waited for; matrix products, arithmetic and copies ran while one was open for 0% of the time, Pallas kernels for 7%

profile of v2, /device:TPU:15, one launch (start us, length us, event | category | flops | bytes accessed | tf_op | source)
XLA Modules:
  0.0 29.4 jit_solution(16481655919576451594)
XLA Ops:
  0.6 0.7 %shard_map.86 = (f32[16,128]{1,0:T(8,128)S(1)}, f32[3,512]{1,0:T(4,128)S(1)}, s32[1,256]{1,0:T(1,128)S(1)}) custom-call(f32[8,128]{1,0:T(8,128)} %direction.1, f32[3,512]{1,0:T(4,128)} %velocity.1, s32[1,256]{1,0:T(1,128)} %bitcast.2), custom_call_target="tpu_custom_call" | custom-call | tf_op jit(solution)/shard_map/pallas_call | solution.py:412
  1.4 0.7 %collective-permute-start = (f32[16,128]{1,0:T(8,128)S(1)}, f32[16,128]{1,0:T(8,128)S(1)}, u32[]{:S(2)}, u32[]{:S(2)}) collective-permute-start(f32[16,128]{1,0:T(8,128)S(1)} %get-tuple-element.24.held), channel_id=1, source_target_pairs={{0,1},{1,0},{2,3},{3,2},{4,5},{5,4},{6,7},{7,6},{8,9},{9,8},{10,11... | collective-permute-start | bytes 24584 | tf_op jit(solution)/shard_map/ppermute | solution.py:425
  2.1 0.8 %collective-permute-done.got.refs_1_ = f32[16,128]{1,0:T(8,128)S(1)} collective-permute-done((f32[16,128]{1,0:T(8,128)S(1)}, f32[16,128]{1,0:T(8,128)S(1)}, u32[]{:S(2)}, u32[]{:S(2)}) %collective-permute-start) | collective-permute-done | bytes 8224 | tf_op jit(solution)/shard_map/ppermute | solution.py:425
  3.0 1.5 %collective-permute-start.3 = (f32[24,128]{1,0:T(8,128)S(1)}, f32[24,128]{1,0:T(8,128)S(1)}, u32[]{:S(2)}, u32[]{:S(2)}) collective-permute-start(f32[24,128]{1,0:T(8,128)S(1)} %shard_map.87.after.refs_0_), channel_id=1, source_target_pairs={{3,6},{6,3},{0,1},{1,2},{2,0},{7,10},{10,7},{4,5},{5,4},{11,14},{1... | collective-permute-start | bytes 36872 | tf_op jit(solution)/shard_map/ppermute | solution.py:428
  4.5 0.1 collective-permute-start.2
  4.6 1.6 %collective-permute-start.1 = (f32[24,128]{1,0:T(8,128)S(1)}, f32[24,128]{1,0:T(8,128)S(1)}, u32[]{:S(2)}, u32[]{:S(2)}) collective-permute-start(f32[24,128]{1,0:T(8,128)S(1)} %shard_map.87.after.refs_0_), channel_id=1, source_target_pairs={{0,3},{1,2},{2,1},{3,0},{4,7},{5,6},{6,5},{7,4},{8,11},{9,10},{10,... | collective-permute-start | bytes 36872 | tf_op jit(solution)/shard_map/ppermute | solution.py:425
  6.8 2.0 %shard_map.88 = (f32[81,81,128]{2,1,0:T(8,128)S(1)}, s32[27,128]{1,0:T(8,128)S(1)}, f32[3,512]{1,0:T(4,128)S(1)}, bf16[256,3456]{1,0:T(8,128)(2,1)S(1)}) custom-call(f32[24,128]{1,0:T(8,128)S(1)} %shard_map.87.after.refs_0_, f32[81,81,128]{2,1,0:T(8,128)} %kmat.1, s32[27,128]{1,0:T(8,128)} %conn.1, f32[3,512]{1,0:T(4,128)} %weight.1), custom_call_target="tpu_custom_call" | custom-call | bytes 8388608 | tf_op jit(solution)/shard_map/pallas_call | solution.py:412
  8.8 0.0 collective-permute-done.3.refs_4_
  8.8 0.6 %collective-permute-done.2.refs_3_ = f32[24,128]{1,0:T(8,128)S(1)} collective-permute-done((f32[24,128]{1,0:T(8,128)S(1)}, f32[24,128]{1,0:T(8,128)S(1)}, u32[]{:S(2)}, u32[]{:S(2)}) %collective-permute-start.2) | collective-permute-done | bytes 12320 | tf_op jit(solution)/shard_map/ppermute | solution.py:428
  9.4 0.0 collective-permute-done.1.refs_2_
  9.4 3.1 %shard_map.89 = (f32[24,768]{1,0:T(8,128)S(1)}, f32[32,256]{1,0:T(8,128)S(1)}, f32[8,128]{1,0:T(8,128)S(1)}, f32[32,256]{1,0:T(8,128)S(1)}, f32[32,256]{1,0:T(8,128)S(1)}) custom-call(f32[24,128]{1,0:T(8,128)S(1)} %shard_map.87.after.refs_0_, f32[16,128]{1,0:T(8,128)S(1)} %collective-permute-done.got.refs_1_, f32[24,128]{1,0:T(8,128)S(1)} %collective-permute-done.1.refs_2_, ...), custom_call_target="tpu_custom_call" | custom-call | tf_op jit(solution)/shard_map/pallas_call | solution.py:412
  12.5 1.8 %collective-permute-start.4 = (f32[32,256]{1,0:T(8,128)S(1)}, f32[32,256]{1,0:T(8,128)S(1)}, u32[]{:S(2)}, u32[]{:S(2)}) collective-permute-start(f32[32,256]{1,0:T(8,128)S(1)} %get-tuple-element.32), channel_id=1, source_target_pairs={{3,4},{4,3},{0,1},{1,2},{2,0},{7,8},{8,7},{5,6},{6,5},{11,12},{12,... | collective-permute-start | bytes 98312 | tf_op jit(solution)/shard_map/ppermute | solution.py:428
  14.3 0.0 collective-permute-start.5
  14.3 0.3 %collective-permute-start.6 = (f32[32,256]{1,0:T(8,128)S(1)}, f32[32,256]{1,0:T(8,128)S(1)}, u32[]{:S(2)}, u32[]{:S(2)}) collective-permute-start(f32[32,256]{1,0:T(8,128)S(1)} %get-tuple-element.35), channel_id=1, source_target_pairs={{0,3},{1,2},{2,1},{3,0},{4,7},{5,6},{6,5},{7,4},{8,11},{9,10},{10,... | collective-permute-start | bytes 98312 | tf_op jit(solution)/shard_map/ppermute | solution.py:425
  14.6 3.2 %collective-permute-done.4.refs_1_ = f32[32,256]{1,0:T(8,128)S(1)} collective-permute-done((f32[32,256]{1,0:T(8,128)S(1)}, f32[32,256]{1,0:T(8,128)S(1)}, u32[]{:S(2)}, u32[]{:S(2)}) %collective-permute-start.4) | collective-permute-done | bytes 32800 | tf_op jit(solution)/shard_map/ppermute | solution.py:428
  17.8 0.0 collective-permute-done.5.refs_10_
  17.8 0.5 %collective-permute-done.6.refs_11_ = f32[32,256]{1,0:T(8,128)S(1)} collective-permute-done((f32[32,256]{1,0:T(8,128)S(1)}, f32[32,256]{1,0:T(8,128)S(1)}, u32[]{:S(2)}, u32[]{:S(2)}) %collective-permute-start.6) | collective-permute-done | bytes 32800 | tf_op jit(solution)/shard_map/ppermute | solution.py:425
  18.3 3.5 %shard_map.90 = (f32[24,512]{1,0:T(8,128)S(1)}, f32[40,128]{1,0:T(8,128)S(1)}, f32[40,128]{1,0:T(8,128)S(1)}, f32[16,128]{1,0:T(8,128)S(1)}, f32[16,128]{1,0:T(8,128)S(1)}, /*index=5*/f32[24,128]{1,0:T(8,128)S(1)}) custom-call(f32[24,768]{1,0:T(8,128)S(1)} %get-tuple-element.31.refs_0_, f32[32,256]{1,0:T(8,128)S(1)} %collective-permute-done.4.refs_1_, ...), custom_call_target="tpu_custom_call" | custom-call | tf_op jit(solution)/shard_map/pallas_call | solution.py:412
  21.8 0.1 collective-permute-start.7
  21.8 1.7 %collective-permute-start.8 = (f32[40,128]{1,0:T(8,128)S(1)}, f32[40,128]{1,0:T(8,128)S(1)}, u32[]{:S(2)}, u32[]{:S(2)}) collective-permute-start(f32[40,128]{1,0:T(8,128)S(1)} %get-tuple-element.39), channel_id=1, source_target_pairs={{3,4},{4,3},{0,1},{1,2},{2,0},{7,8},{8,7},{5,6},{6,5},{11,12},{12,... | collective-permute-start | bytes 61448 | tf_op jit(solution)/shard_map/ppermute | solution.py:428
  23.5 0.3 %collective-permute-start.9 = (f32[16,128]{1,0:T(8,128)S(1)}, f32[16,128]{1,0:T(8,128)S(1)}, u32[]{:S(2)}, u32[]{:S(2)}) collective-permute-start(f32[16,128]{1,0:T(8,128)S(1)} %get-tuple-element.40), channel_id=1, source_target_pairs={{3,6},{6,3},{0,1},{1,2},{2,0},{7,10},{10,7},{4,5},{5,4},{11,14},{1... | collective-permute-start | bytes 24584 | tf_op jit(solution)/shard_map/ppermute | solution.py:428
  23.8 3.7 %collective-permute-done.9.refs_3_ = f32[16,128]{1,0:T(8,128)S(1)} collective-permute-done((f32[16,128]{1,0:T(8,128)S(1)}, f32[16,128]{1,0:T(8,128)S(1)}, u32[]{:S(2)}, u32[]{:S(2)}) %collective-permute-start.9) | collective-permute-done | bytes 8224 | tf_op jit(solution)/shard_map/ppermute | solution.py:428
  27.5 0.0 collective-permute-done.7.refs_1_.refs_4_
  27.5 0.0 collective-permute-done.8.refs_2_
  27.5 0.1 collective-permute-start.10
  27.6 1.2 %collective-permute-done.10.refs_3_ = f32[32,128]{1,0:T(8,128)S(1)} collective-permute-done((f32[32,128]{1,0:T(8,128)S(1)}, f32[32,128]{1,0:T(8,128)S(1)}, u32[]{:S(2)}, u32[]{:S(2)}) %collective-permute-start.10) | collective-permute-done | bytes 16416 | tf_op jit(solution)/shard_map/ppermute | solution.py:425
  28.8 0.6 %shard_map.92 = (f32[8,128]{1,0:T(8,128)}, f32[24,512]{1,0:T(8,128)}) custom-call(f32[24,512]{1,0:T(8,128)S(1)} %get-tuple-element.36.refs_0_, f32[8,128]{1,0:T(8,128)S(1)} %get-tuple-element.42.refs_1_, f32[40,128]{1,0:T(8,128)S(1)} %collective-permute-done.8.refs_2_, f32[32,128]{1,0:T(8,128)S(1)} %collective-permute-done.10.refs_3_, ...), custom_call_target="tpu_custom_call" | custom-call | tf_op jit(solution)/shard_map/pallas_call | solution.py:412
  (2 shorter events, 0.0 us)
Async XLA Ops:
  1.4 1.6 %collective-permute-start = (f32[16,128]{1,0:T(8,128)S(1)}, f32[16,128]{1,0:T(8,128)S(1)}, u32[]{:S(2)}, u32[]{:S(2)}) collective-permute-start(f32[16,128]{1,0:T(8,128)S(1)} %get-tuple-element.24.held), channel_id=1, source_target_pairs={{0,1},{1,0},{2,3},{3,2},{4,5},{5,4},{6,7},{7,6},{8,9},{9,8},{10,11... | collective-permute-start | bytes 24584 | tf_op jit(solution)/shard_map/ppermute | solution.py:425
  3.0 5.8 %collective-permute-start.3 = (f32[24,128]{1,0:T(8,128)S(1)}, f32[24,128]{1,0:T(8,128)S(1)}, u32[]{:S(2)}, u32[]{:S(2)}) collective-permute-start(f32[24,128]{1,0:T(8,128)S(1)} %shard_map.87.after.refs_0_), channel_id=1, source_target_pairs={{3,6},{6,3},{0,1},{1,2},{2,0},{7,10},{10,7},{4,5},{5,4},{11,14},{1... | collective-permute-start | bytes 36872 | tf_op jit(solution)/shard_map/ppermute | solution.py:428
  4.5 4.9 %collective-permute-start.2 = (f32[24,128]{1,0:T(8,128)S(1)}, f32[24,128]{1,0:T(8,128)S(1)}, u32[]{:S(2)}, u32[]{:S(2)}) collective-permute-start(f32[24,128]{1,0:T(8,128)S(1)} %shard_map.87.after.refs_0_), channel_id=1, source_target_pairs={{3,4},{4,3},{0,1},{1,2},{2,0},{7,8},{8,7},{5,6},{6,5},{11,12},{12,... | collective-permute-start | bytes 36872 | tf_op jit(solution)/shard_map/ppermute | solution.py:428
  4.6 4.8 %collective-permute-start.1 = (f32[24,128]{1,0:T(8,128)S(1)}, f32[24,128]{1,0:T(8,128)S(1)}, u32[]{:S(2)}, u32[]{:S(2)}) collective-permute-start(f32[24,128]{1,0:T(8,128)S(1)} %shard_map.87.after.refs_0_), channel_id=1, source_target_pairs={{0,3},{1,2},{2,1},{3,0},{4,7},{5,6},{6,5},{7,4},{8,11},{9,10},{10,... | collective-permute-start | bytes 36872 | tf_op jit(solution)/shard_map/ppermute | solution.py:425
  12.5 5.3 %collective-permute-start.4 = (f32[32,256]{1,0:T(8,128)S(1)}, f32[32,256]{1,0:T(8,128)S(1)}, u32[]{:S(2)}, u32[]{:S(2)}) collective-permute-start(f32[32,256]{1,0:T(8,128)S(1)} %get-tuple-element.32), channel_id=1, source_target_pairs={{3,4},{4,3},{0,1},{1,2},{2,0},{7,8},{8,7},{5,6},{6,5},{11,12},{12,... | collective-permute-start | bytes 98312 | tf_op jit(solution)/shard_map/ppermute | solution.py:428
  14.3 3.5 %collective-permute-start.5 = (f32[32,256]{1,0:T(8,128)S(1)}, f32[32,256]{1,0:T(8,128)S(1)}, u32[]{:S(2)}, u32[]{:S(2)}) collective-permute-start(f32[32,256]{1,0:T(8,128)S(1)} %get-tuple-element.34), channel_id=1, source_target_pairs={{0,1},{1,0},{2,3},{3,2},{4,5},{5,4},{6,7},{7,6},{8,9},{9,8},{10,11... | collective-permute-start | bytes 98312 | tf_op jit(solution)/shard_map/ppermute | solution.py:425
  14.3 4.0 %collective-permute-start.6 = (f32[32,256]{1,0:T(8,128)S(1)}, f32[32,256]{1,0:T(8,128)S(1)}, u32[]{:S(2)}, u32[]{:S(2)}) collective-permute-start(f32[32,256]{1,0:T(8,128)S(1)} %get-tuple-element.35), channel_id=1, source_target_pairs={{0,3},{1,2},{2,1},{3,0},{4,7},{5,6},{6,5},{7,4},{8,11},{9,10},{10,... | collective-permute-start | bytes 98312 | tf_op jit(solution)/shard_map/ppermute | solution.py:425
  21.8 5.8 %collective-permute-start.7 = (f32[40,128]{1,0:T(8,128)S(1)}, f32[40,128]{1,0:T(8,128)S(1)}, u32[]{:S(2)}, u32[]{:S(2)}) collective-permute-start(f32[40,128]{1,0:T(8,128)S(1)} %get-tuple-element.38), channel_id=1, source_target_pairs={{0,3},{1,2},{2,1},{3,0},{4,7},{5,6},{6,5},{7,4},{8,11},{9,10},{10,... | collective-permute-start | bytes 61448 | tf_op jit(solution)/shard_map/ppermute | solution.py:425
  21.8 5.7 %collective-permute-start.8 = (f32[40,128]{1,0:T(8,128)S(1)}, f32[40,128]{1,0:T(8,128)S(1)}, u32[]{:S(2)}, u32[]{:S(2)}) collective-permute-start(f32[40,128]{1,0:T(8,128)S(1)} %get-tuple-element.39), channel_id=1, source_target_pairs={{3,4},{4,3},{0,1},{1,2},{2,0},{7,8},{8,7},{5,6},{6,5},{11,12},{12,... | collective-permute-start | bytes 61448 | tf_op jit(solution)/shard_map/ppermute | solution.py:428
  23.5 4.0 %collective-permute-start.9 = (f32[16,128]{1,0:T(8,128)S(1)}, f32[16,128]{1,0:T(8,128)S(1)}, u32[]{:S(2)}, u32[]{:S(2)}) collective-permute-start(f32[16,128]{1,0:T(8,128)S(1)} %get-tuple-element.40), channel_id=1, source_target_pairs={{3,6},{6,3},{0,1},{1,2},{2,0},{7,10},{10,7},{4,5},{5,4},{11,14},{1... | collective-permute-start | bytes 24584 | tf_op jit(solution)/shard_map/ppermute | solution.py:428
  27.5 1.2 %collective-permute-start.10 = (f32[32,128]{1,0:T(8,128)S(1)}, f32[32,128]{1,0:T(8,128)S(1)}, u32[]{:S(2)}, u32[]{:S(2)}) collective-permute-start(f32[32,128]{1,0:T(8,128)S(1)} %get-tuple-element.43), channel_id=1, source_target_pairs={{0,1},{1,0},{2,3},{3,2},{4,5},{5,4},{6,7},{7,6},{8,9},{9,8},{10,11... | collective-permute-start | bytes 49160 | tf_op jit(solution)/shard_map/ppermute | solution.py:425
